TPU v7x, 512 devices: a whole 4x4x16 slice. The times are simulated.
512 devices in a mesh: pipe: 8 (over x, y_hi), ctx: 64 (over z, y_lo, core).
Axes of the slice: x: 4, y: 4 (y_hi: 2, y_lo: 2; y = y_hi * 2 + y_lo), z: 16, core: 2. Of those that a mesh axis runs over, the one named last changes fastest.
Arguments:
- saved_in: bfloat16 [8, 8192, 2048], P('pipe', 'ctx'), may hold values from -20 to 20, as said below
- grad_in: bfloat16 [8, 8192, 2048], P('pipe', 'ctx'), may hold values from -6 to 6
- queries: bfloat16 [8, 8192, 2048], P('pipe', 'ctx'), may hold values from -60 to 60
- d_heads: bfloat16 [8, 8192, 2048], P('pipe', 'ctx'), may hold values from -6 to 6
- kv_weights: bfloat16 [8, 2048, 512], P('pipe', 'ctx'), may hold values from -0.125 to 0.125
Outputs:
- grad_out: bfloat16 [8, 8192, 2048], P('pipe', 'ctx')
- d_queries: bfloat16 [8, 8192, 2048], P('pipe', 'ctx')
- weight_grad: float32 [8, 2048, 512], P('pipe', 'ctx')
Inputs may be any that keep to these rules, and one draw needn't show every extreme that they name: `saved_in`: stored layer activations.
All inputs are finite; a program needn't handle non-finite values.
Results may differ from a plain program's by a relative error of at most 0.0039.
The roundings to bfloat16 on the way count: a program that leaves them out, or rounds other values in their place, can miss the bound.
Values may be sent and summed in bfloat16 or wider, within the bound.
A program may use at most 64 MiB of HBM per device.

v0:
```python
import math

import jax
import jax.numpy as jnp
from jax import lax
from jax.sharding import PartitionSpec as P

HEAD_DIM = 128
KV_HEADS = 2


epsilon = 1e-06


def shifted(block, axis, distance):
    devices = range(lax.axis_size(axis))
    route = [((i - distance) % len(devices), i) for i in devices]
    return lax.ppermute(block, axis, route)


def padded(cells, sides, width):
    for axis, dim in sides:
        count = lax.axis_size(axis)
        head = lax.slice_in_dim(cells, 0, width, axis=dim)
        tail = lax.slice_in_dim(cells, cells.shape[dim] - width, cells.shape[dim], axis=dim)
        cells = jnp.concatenate(
            [
                lax.ppermute(tail, axis, [(i, (i + 1) % count) for i in range(count)]),
                cells,
                lax.ppermute(head, axis, [((i + 1) % count, i) for i in range(count)]),
            ],
            axis=dim,
        )
    return cells


def window_mask(row_count):
    query_pos = lax.broadcasted_iota(jnp.int32, (row_count, 3 * row_count), 0)
    key_pos = lax.broadcasted_iota(jnp.int32, (row_count, 3 * row_count), 1)
    offset = key_pos - query_pos
    return (offset >= 0) & (offset <= 2 * row_count)


def per_device(saved_in, grad_in, queries, d_heads, kv_weights):
    upstream = shifted(grad_in, "pipe", -1)[0]
    kv_matrix = lax.all_gather(kv_weights[0], "ctx", axis=0, tiled=True)
    saved = saved_in[0]
    row_count, model_width = saved.shape
    kv_width = kv_matrix.shape[1] // 2
    groups = KV_HEADS
    head_dim = HEAD_DIM
    per_group = model_width // (groups * head_dim)
    score_scale = 1.0 / math.sqrt(head_dim)
    highest = lax.Precision.HIGHEST
    saved_wide = saved.astype(jnp.float32)
    factor = lax.rsqrt(jnp.mean(saved_wide * saved_wide, axis=-1, keepdims=True) + epsilon)
    normed = saved_wide * factor
    normed_b = normed.astype(jnp.bfloat16)
    kv_rows = jnp.dot(normed_b, kv_matrix, preferred_element_type=jnp.float32).astype(jnp.bfloat16)
    wide_kv = padded(kv_rows, (("ctx", 0),), row_count)
    key_rows = wide_kv[:, :kv_width].reshape(3 * row_count, groups, head_dim)
    value_rows = wide_kv[:, kv_width:].reshape(3 * row_count, groups, head_dim)
    own_query = queries[0].reshape(row_count, groups, per_group, head_dim)
    grad_heads = d_heads[0].reshape(row_count, groups, per_group, head_dim)
    valid = window_mask(row_count)[None, None]
    scores = (
        jnp.einsum("qgne,kge->gnqk", own_query, key_rows, preferred_element_type=jnp.float32)
        * score_scale
    )
    scores = jnp.where(valid, scores, -1e30)
    row_peak = jnp.max(scores, axis=-1, keepdims=True)
    lifted = jnp.exp(scores - row_peak)
    row_total = jnp.sum(lifted, axis=-1, keepdims=True)
    probs = lifted / row_total
    d_probs = jnp.einsum(
        "qgne,kge->gnqk", grad_heads, value_rows, preferred_element_type=jnp.float32
    )
    row_dot = jnp.sum(probs * d_probs, axis=-1, keepdims=True)
    d_scores = (probs * (d_probs - row_dot) * score_scale).astype(jnp.bfloat16)
    d_queries = (
        jnp.einsum("gnqk,kge->qgne", d_scores, key_rows, preferred_element_type=jnp.float32)
        .astype(jnp.bfloat16)
        .reshape(row_count, model_width)
    )
    row_stats = jnp.stack([row_peak[..., 0], row_total[..., 0], row_dot[..., 0]])
    row_stats = jnp.transpose(row_stats, (0, 3, 1, 2)).reshape(3, row_count, groups * per_group)
    wide_stats = padded(row_stats, (("ctx", 1),), row_count)
    wide_stats = jnp.transpose(
        wide_stats.reshape(3, 3 * row_count, groups, per_group), (0, 2, 3, 1)
    )
    query_pair = jnp.stack([queries[0], d_heads[0]])
    wide_pair = padded(query_pair, (("ctx", 1),), row_count)
    wide_query = wide_pair[0].reshape(3 * row_count, groups, per_group, head_dim)
    wide_grad = wide_pair[1].reshape(3 * row_count, groups, per_group, head_dim)
    own_keys = kv_rows[:, :kv_width].reshape(row_count, groups, head_dim)
    own_values = kv_rows[:, kv_width:].reshape(row_count, groups, head_dim)
    key_scores = (
        jnp.einsum("qgne,kge->gnkq", wide_query, own_keys, preferred_element_type=jnp.float32)
        * score_scale
    )
    key_lifted = jnp.exp(key_scores - wide_stats[0][:, :, None, :])
    key_probs = jnp.where(valid, key_lifted / wide_stats[1][:, :, None, :], 0.0)
    key_probs_b = key_probs.astype(jnp.bfloat16)
    key_dprobs = jnp.einsum(
        "qgne,kge->gnkq", wide_grad, own_values, preferred_element_type=jnp.float32
    )
    key_dscores = (key_probs * (key_dprobs - wide_stats[2][:, :, None, :]) * score_scale).astype(
        jnp.bfloat16
    )
    d_keys = jnp.einsum(
        "gnkq,qgne->kge", key_dscores, wide_query, preferred_element_type=jnp.float32
    ).reshape(row_count, kv_width)
    d_values = jnp.einsum(
        "gnkq,qgne->kge", key_probs_b, wide_grad, preferred_element_type=jnp.float32
    ).reshape(row_count, kv_width)
    d_kv = jnp.concatenate([d_keys, d_values], axis=1)
    d_normed = jnp.dot(d_kv, kv_matrix.astype(jnp.float32).T, precision=highest)
    upstream_wide = upstream.astype(jnp.float32)
    grad_out = (
        upstream_wide
        + factor * (d_normed - normed * jnp.mean(d_normed * normed, axis=-1, keepdims=True))
    ).astype(jnp.bfloat16)
    terms = jnp.dot(normed_b.astype(jnp.float32).T, d_kv, precision=highest)
    total_tokens = row_count * lax.axis_size("ctx")
    weight_grad = lax.psum_scatter(terms, "ctx", scatter_dimension=0, tiled=True) * (
        1.0 / math.sqrt(total_tokens)
    )
    return (grad_out[None], d_queries[None], weight_grad[None])


def solution(mesh):
    in_specs = (
        P("pipe", "ctx", None),
        P("pipe", "ctx", None),
        P("pipe", "ctx", None),
        P("pipe", "ctx", None),
        P("pipe", "ctx", None),
    )
    out_specs = (P("pipe", "ctx", None), P("pipe", "ctx", None), P("pipe", "ctx", None))
    return jax.shard_map(
        per_device, mesh=mesh, in_specs=in_specs, out_specs=out_specs, check_vma=False
    )
```

profile of v0, /device:TPU:1, one launch (start us, length us, event | category | flops | bytes accessed | tf_op | source)
XLA Modules:
  0.0 416.7 jit_solution(1812704303039384591)
XLA Ops:
  7.2 0.7 all-gather.3.cloned.1.call-update
  8.0 1.4 copy.19
  9.3 1.3 copy.20
  10.8 8.7 %collective-permute-start.2 = (bf16[2,128,2048]{1,2,0:T(8,128)(2,1)S(1)}, bf16[2,128,2048]{1,2,0:T(8,128)(2,1)S(1)}, u32[]{:S(2)}, u32[]{:S(2)}) collective-permute-start(bf16[2,128,2048]{1,2,0:T(8,128)(2,1)S(1)} %pad_maximum_fusion.1), channel_id=1, source_target_pairs={{1,0},{2,1},{3,2},{4,3},{5,4},{6,5},{7,6},{8,7},{9,8},{10,9},{11,1... | collective-permute-start | bytes 3145736 | tf_op jit(solution)/shard_map/ppermute | solution.py:30
  19.5 1.9 collective-permute-start.1
  21.5 0.9 copy.50
  22.5 0.7 fusion.51
  23.3 4.5 %collective-permute-done.2 = bf16[2,128,2048]{1,2,0:T(8,128)(2,1)S(1)} collective-permute-done((bf16[2,128,2048]{1,2,0:T(8,128)(2,1)S(1)}, bf16[2,128,2048]{1,2,0:T(8,128)(2,1)S(1)}, u32[]{:S(2)}, u32[]{:S(2)}) %collective-permute-start.2) | collective-permute-done | bytes 1048608 | tf_op jit(solution)/shard_map/ppermute | solution.py:30
  27.8 11.9 %collective-permute-done.1 = bf16[2,128,2048]{1,2,0:T(8,128)(2,1)S(1)} collective-permute-done((bf16[2,128,2048]{1,2,0:T(8,128)(2,1)S(1)}, bf16[2,128,2048]{1,2,0:T(8,128)(2,1)S(1)}, u32[]{:S(2)}, u32[]{:S(2)}) %collective-permute-start.1) | collective-permute-done | bytes 1048608 | tf_op jit(solution)/shard_map/ppermute | solution.py:28
  39.8 1.9 pad_maximum_fusion
  41.7 96.4 %all-gather.3.cloned.1.call-done = bf16[1,2048,512]{2,1,0:T(8,128)(2,1)} async-done(((bf16[1,32,512]{2,1,0:T(8,128)(2,1)}), bf16[1,2048,512]{2,1,0:T(8,128)(2,1)}) %all-gather.3.cloned.1.call-update) | async-done | bytes 2097168 | tf_op jit(solution)/shard_map/all_gather | solution.py:46
  138.1 2.1 fusion.30
  140.1 2.2 collective-permute-start.4
  142.3 3.4 collective-permute-start.3
  145.7 3.4 fusion.62
  149.5 1.6 fusion.12
  151.2 1.1 fusion.11
  152.3 2.7 fusion.3
  155.0 5.8 %collective-permute-start.6 = (f32[3,128,16]{1,2,0:T(8,128)S(1)}, f32[3,128,16]{1,2,0:T(8,128)S(1)}, u32[]{:S(2)}, u32[]{:S(2)}) collective-permute-start(f32[3,128,16]{1,2,0:T(8,128)S(1)} %get-tuple-element.19), channel_id=1, source_target_pairs={{1,0},{2,1},{3,2},{4,3},{5,4},{6,5},{7,6},{8,7},{9,8},{10,9},{11,1... | collective-permute-start | bytes 73736 | tf_op jit(solution)/shard_map/ppermute | solution.py:30
  160.8 1.9 collective-permute-start.5
  162.8 1.3 collective-permute-done.5
  164.2 2.3 fusion.9
  166.6 1.7 copy-done.1
  168.9 3.4 fusion.23
  172.3 3.9 fusion.45
  176.2 6.7 %collective-permute-start = (bf16[1,128,2048]{2,1,0:T(8,128)(2,1)}, bf16[1,128,2048]{2,1,0:T(8,128)(2,1)}, u32[]{:S(2)}, u32[]{:S(2)}) collective-permute-start(bf16[1,128,2048]{2,1,0:T(8,128)(2,1)} %param.6), channel_id=1, source_target_pairs={{64,0},{128,64},{192,128},{256,192},{320,256},{384,320},{448,384},... | collective-permute-start | bytes 1572872 | tf_op jit(solution)/shard_map/ppermute | solution.py:18
  182.9 5.3 %fusion.27 = bf16[2,128,8,128]{3,1,2,0:T(8,128)(2,1)} fusion(bf16[384,2,128,1]{0,2,3,1:T(8,128)(2,1)S(1)} %copy.40, f32[2,384,128,8]{1,2,3,0:T(8,128)} %get-tuple-element.23, f32[2,8,128]{2,1,0:T(8,128)S(1)} %get-tuple-element.22, f32[2,384,128,8]{1,2,3,0:T(8,128)} %copy-done.2, f32[2,8,128]{2,1,0:T(8,128)S(1)} %fusion.11, ...), kind=kOutput, calls=%fused_computation.35 | convolution fusion | flops 207880192 | bytes 7086080 | tf_op jit(solution)/shard_map/gnqk,kge->qgne/dot_general | solution.py:81
  188.1 2.0 copy.30
  190.2 2.0 fusion.33
  192.2 2.2 fusion.39
  194.4 214.0 %reduce-scatter.2.cloned.1.call-done = f32[32,512]{1,0:T(8,128)} async-done(((f32[2048,512]{1,0:T(8,128)}), f32[32,512]{1,0:T(8,128)}) %reduce-scatter.2.cloned.1.call-update) | async-done | bytes 65552 | tf_op jit(solution)/shard_map/reduce_scatter | solution.py:125
  408.4 1.5 multiply_bitcast_fusion
  (41 shorter events, 1.6 us)
Async XLA Ops:
  7.2 15.2 %copy-start.5 = (bf16[1,128,2048]{2,1,0:T(8,128)(2,1)S(1)}, bf16[1,128,2048]{2,1,0:T(8,128)(2,1)}, u32[]{:S(2)}) copy-start(bf16[1,128,2048]{2,1,0:T(8,128)(2,1)} %param.7) | copy-start | bytes 1572868
  7.2 14.3 %copy-start.4 = (bf16[1,128,2048]{2,1,0:T(8,128)(2,1)S(1)}, bf16[1,128,2048]{2,1,0:T(8,128)(2,1)}, u32[]{:S(2)}) copy-start(bf16[1,128,2048]{2,1,0:T(8,128)(2,1)} %param.8) | copy-start | bytes 1572868
  7.2 130.9 %all-gather.3.cloned.1.call-start = ((), (), s32[]{:S(2)}) async-start(), calls=%async_computation.2 | async-start | bytes 2129920 | tf_op jit(solution)/shard_map/all_gather | solution.py:46
  7.9 15.2 %copy-start = (bf16[1,128,2048]{2,1,0:T(8,128)(2,1)S(1)}, bf16[1,128,2048]{2,1,0:T(8,128)(2,1)}, u32[]{:S(2)}) copy-start(bf16[1,128,2048]{2,1,0:T(8,128)(2,1)} %param.5) | copy-start | bytes 1572868
  7.9 400.5 %reduce-scatter.2.cloned.1.call-start = ((), (), s32[]{:S(2)}) async-start(), calls=%async_computation.1 | async-start | bytes 4259840 | tf_op jit(solution)/shard_map/reduce_scatter | solution.py:125
  10.8 17.1 %collective-permute-start.2 = (bf16[2,128,2048]{1,2,0:T(8,128)(2,1)S(1)}, bf16[2,128,2048]{1,2,0:T(8,128)(2,1)S(1)}, u32[]{:S(2)}, u32[]{:S(2)}) collective-permute-start(bf16[2,128,2048]{1,2,0:T(8,128)(2,1)S(1)} %pad_maximum_fusion.1), channel_id=1, source_target_pairs={{1,0},{2,1},{3,2},{4,3},{5,4},{6,5},{7,6},{8,7},{9,8},{10,9},{11,1... | collective-permute-start | bytes 3145736 | tf_op jit(solution)/shard_map/ppermute | solution.py:30
  19.5 20.2 %collective-permute-start.1 = (bf16[2,128,2048]{1,2,0:T(8,128)(2,1)S(1)}, bf16[2,128,2048]{1,2,0:T(8,128)(2,1)S(1)}, u32[]{:S(2)}, u32[]{:S(2)}) collective-permute-start(bf16[2,128,2048]{1,2,0:T(8,128)(2,1)S(1)} %pad_maximum_fusion.1), channel_id=1, source_target_pairs={{0,1},{1,2},{2,3},{3,4},{4,5},{5,6},{6,7},{7,8},{8,9},{9,10},{10,1... | collective-permute-start | bytes 3145736 | tf_op jit(solution)/shard_map/ppermute | solution.py:28
  140.1 9.0 %collective-permute-start.4 = (bf16[128,512]{1,0:T(8,128)(2,1)S(1)}, bf16[128,512]{1,0:T(8,128)(2,1)S(1)}, u32[]{:S(2)}, u32[]{:S(2)}) collective-permute-start(bf16[128,512]{1,0:T(8,128)(2,1)S(1)} %fusion.30), channel_id=1, source_target_pairs={{1,0},{2,1},{3,2},{4,3},{5,4},{6,5},{7,6},{8,7},{9,8},{10,9},{11,1... | collective-permute-start | bytes 393224 | tf_op jit(solution)/shard_map/ppermute | solution.py:30
  142.3 6.8 %collective-permute-start.3 = (bf16[128,512]{1,0:T(8,128)(2,1)S(1)}, bf16[128,512]{1,0:T(8,128)(2,1)S(1)}, u32[]{:S(2)}, u32[]{:S(2)}) collective-permute-start(bf16[128,512]{1,0:T(8,128)(2,1)S(1)} %fusion.30), channel_id=1, source_target_pairs={{0,1},{1,2},{2,3},{3,4},{4,5},{5,6},{6,7},{7,8},{8,9},{9,10},{10,1... | collective-permute-start | bytes 393224 | tf_op jit(solution)/shard_map/ppermute | solution.py:28
  149.2 2.0 copy-start.7
  149.5 2.8 copy-start.6
  151.1 3.8 copy-start.2
  155.0 7.8 %collective-permute-start.6 = (f32[3,128,16]{1,2,0:T(8,128)S(1)}, f32[3,128,16]{1,2,0:T(8,128)S(1)}, u32[]{:S(2)}, u32[]{:S(2)}) collective-permute-start(f32[3,128,16]{1,2,0:T(8,128)S(1)} %get-tuple-element.19), channel_id=1, source_target_pairs={{1,0},{2,1},{3,2},{4,3},{5,4},{6,5},{7,6},{8,7},{9,8},{10,9},{11,1... | collective-permute-start | bytes 73736 | tf_op jit(solution)/shard_map/ppermute | solution.py:30
  160.8 3.4 collective-permute-start.5
  166.6 1.7 copy-start.1
  176.1 6.7 %copy-start.8 = (pred[128,384]{1,0:T(8,128)(4,1)S(1)}, pred[128,384]{1,0:T(8,128)(4,1)}, u32[]{:S(2)}) copy-start(pred[128,384]{1,0:T(8,128)(4,1)} %fusion.51) | copy-start | bytes 147460
  176.2 16.0 %collective-permute-start = (bf16[1,128,2048]{2,1,0:T(8,128)(2,1)}, bf16[1,128,2048]{2,1,0:T(8,128)(2,1)}, u32[]{:S(2)}, u32[]{:S(2)}) collective-permute-start(bf16[1,128,2048]{2,1,0:T(8,128)(2,1)} %param.6), channel_id=1, source_target_pairs={{64,0},{128,64},{192,128},{256,192},{320,256},{384,320},{448,384},... | collective-permute-start | bytes 1572872 | tf_op jit(solution)/shard_map/ppermute | solution.py:18
  182.9 7.3 %copy-start.3 = (bf16[1,2048,512]{2,1,0:T(8,128)(2,1)S(1)}, bf16[1,2048,512]{2,1,0:T(8,128)(2,1)}, u32[]{:S(2)}) copy-start(bf16[1,2048,512]{2,1,0:T(8,128)(2,1)} %all-gather.3.cloned.1.call-done) | copy-start | bytes 6291460
Sparse Core Ops, SparseCore 0:
  10.1 127.8 all-gather.2
  176.3 232.1 reduce-scatter.1
where the time goes:
time: 421 us; the launch traced here: 417 us
  waiting for transfers between devices  329 us (78%)
  starting transfers between devices  30.8 us (7%)
  matrix products  23.8 us (6%)
  between operations  14.3 us (3%)
  local copies, waits for them, and re-layouts  11.2 us (3%)
  other arithmetic  7.75 us (2%)
    reduce_scatter x1, waiting for transfers between devices, per_device(): lax.psum_scatter(terms, 'ctx', scatter_dimension=0, tiled=True)  214 us
    all_gather x1, waiting for transfers between devices, per_device(): kv_matrix = lax.all_gather(kv_weights[0], 'ctx', axis=0, tiled=True)  96.4 us
    ppermute x3, starting transfers between devices, padded(): lax.ppermute(head, axis, [((i + 1) % count, i) for i in range(count)])  16.8 us
    ppermute x3, waiting for transfers between devices, padded(): lax.ppermute(tail, axis, [(i, (i + 1) % count) for i in range(count)])  13.3 us
  transfers between devices with their start and end apart: 9, of which 5 were waited for; matrix products, arithmetic and copies ran while one was open for 5% of the time, Pallas kernels for 0%

commit v1 on v0

v1 whole, which is shorter than its diff:
```python
import functools
import math

import jax
import jax.numpy as jnp
from jax import lax
from jax.experimental import pallas as pl
from jax.experimental.pallas import tpu as pltpu
from jax.sharding import PartitionSpec as P

HEADS = 16
HEAD_DIM = 128
KV_HEADS = 2
PER_GROUP = HEADS // KV_HEADS
LANES = 4
EPSILON = 1e-06

F32 = jnp.float32
BF16 = jnp.bfloat16
NT = (((1,), (1,)), ((), ()))


def dot(a, b, dims=(((1,), (0,)), ((), ()))):
    return lax.dot_general(a, b, dims, preferred_element_type=F32)


def kernel(
    n_pipe, n_ctx,
    z_ref, up_ref, q_ref, g_ref, w_ref,
    go_ref, dq_ref, wg_ref,
    z_v, q_v, g_v, up_v, go_v, dq_v, wg_v,
    nb, fac, nt, nt_sh, w_v, kvw, acc,
    dkw, fold, dkv_hi, dkv_lo, dkv_sh, prod, dn, dot_sum,
    p_snd, p_rcv, m_snd, m_rcv,
    loc_sem, out_sem,
    ag_recv, ag_zp, ag_zm, ag_y, ag_c, ag_yc,
    nt_snd, nt_rcv, up_snd, up_rcv,
    halo_snd, halo_rcv, fold_snd, fold_rcv,
    sh_snd, sh_rcv, shf_snd,
    ps_snd, ps_rcv, ms_snd, ms_rcv,
):
    rows = z_v.shape[0]
    zs = n_ctx // LANES
    hp = zs // 2
    hm = zs - 1 - hp
    feats = w_ref.shape[0]
    width = LANES * feats
    scale = 1.0 / math.sqrt(HEAD_DIM)

    pipe = lax.axis_index("pipe")
    ctx = lax.axis_index("ctx")
    z = ctx // LANES
    lane = lax.rem(ctx, LANES)
    y = lane // 2
    core = lax.rem(lane, 2)
    lane_c = 2 * y + (1 - core)
    lane_y = 2 * (1 - y) + core
    lane_d = 2 * (1 - y) + (1 - core)

    def at_z(distance):
        return lax.rem(z + distance + zs, zs)

    def dev(zz, ll):
        return zz * LANES + ll

    z_next, z_prev = dev(at_z(1), lane), dev(at_z(-1), lane)
    me_c, me_y, me_d = dev(z, lane_c), dev(z, lane_y), dev(z, lane_d)
    right = lax.rem(ctx + 1, n_ctx)
    left = lax.rem(ctx + n_ctx - 1, n_ctx)
    pipe_prev = lax.rem(pipe + n_pipe - 1, n_pipe)
    pipe_next = lax.rem(pipe + 1, n_pipe)

    def remote(src, dst, snd, rcv, to, to_pipe=None):
        return pltpu.make_async_remote_copy(
            src_ref=src, dst_ref=dst, send_sem=snd, recv_sem=rcv,
            device_id=(pipe if to_pipe is None else to_pipe, to),
            device_id_type=pl.DeviceIdType.MESH,
        )

    loads = [
        pltpu.make_async_copy(z_ref, z_v, loc_sem.at[0]),
        pltpu.make_async_copy(
            w_ref, w_v.at[pl.ds(pl.multiple_of(ctx * feats, feats), feats)], loc_sem.at[1]
        ),
        pltpu.make_async_copy(q_ref, q_v, loc_sem.at[2]),
        pltpu.make_async_copy(g_ref, g_v, loc_sem.at[3]),
    ]
    for load in loads:
        load.start()

    barrier = pltpu.get_barrier_semaphore()
    greeted = [(pipe, d) for d in (z_next, z_prev, me_c, me_y, me_d, right, left)]
    if n_pipe > 1:
        greeted += [(pipe_prev, ctx), (pipe_next, ctx)]
    for who in greeted:
        pl.semaphore_signal(barrier, inc=1, device_id=who, device_id_type=pl.DeviceIdType.MESH)
    pl.semaphore_wait(barrier, len(greeted))

    def piece_at(zz, ll):
        start = pl.multiple_of((zz * LANES + ll) * feats, feats)
        return w_v.at[pl.ds(start, feats)], ag_recv.at[zz * LANES + ll]

    def push(zz, ll, to, snd, own=False):
        dst, rcv = piece_at(zz, ll)
        return remote(w_ref if own else dst, dst, snd.at[zz], rcv, to)

    def arrive(zz, ll):
        dst, rcv = piece_at(zz, ll)
        remote(dst, dst, ag_yc.at[zz], rcv, me_c).wait_recv()

    pushes = []

    def start(copy):
        copy.start()
        pushes.append(copy)

    start(push(z, lane, z_next, ag_zp, own=True))
    if hm > 0:
        start(push(z, lane, z_prev, ag_zm, own=True))
    start(push(z, lane, me_y, ag_y, own=True))
    start(push(z, lane, me_c, ag_c, own=True))

    loads[0].wait()
    z_wide = z_v[...].astype(F32)
    factor = lax.rsqrt(jnp.mean(z_wide * z_wide, axis=-1, keepdims=True) + EPSILON)
    fac[...] = jnp.broadcast_to(factor, fac.shape)
    nb[...] = (z_wide * factor).astype(BF16)
    for k in range(zs):
        block = nb[:, k * width:(k + 1) * width].astype(F32)
        nt[k] = block.T.astype(BF16).reshape(LANES, feats, rows)

    for i, (ll, to) in enumerate(((lane_c, me_c), (lane_y, me_y), (lane_d, me_d))):
        start(remote(nt.at[:, ll], nt_sh.at[lane], nt_snd.at[i], nt_rcv.at[lane], to))
    nt_sh[lane] = nt[:, lane]
    loads[1].wait()
    acc[...] = jnp.zeros_like(acc)

    def project(zz):
        at = pl.multiple_of(zz * width, width)
        acc[...] += dot(nb[:, pl.ds(at, width)], w_v[pl.ds(at, width), :])

    def slices(s):
        if s == 0:
            return [z]
        return ([at_z(-s)] if s <= hp else []) + ([at_z(s)] if s <= hm else [])

    for s in range(1, hp + 3):
        if s <= hp:
            zz = at_z(-s)
            arrive(zz, lane)
            if s < hp:
                start(push(zz, lane, z_next, ag_zp))
            start(push(zz, lane, me_y, ag_y))
            start(push(zz, lane, me_c, ag_c))
        if s <= hm:
            zz = at_z(s)
            arrive(zz, lane)
            if s < hm:
                start(push(zz, lane, z_prev, ag_zm))
            start(push(zz, lane, me_y, ag_y))
            start(push(zz, lane, me_c, ag_c))
        if 1 <= s <= hp + 1:
            for zz in slices(s - 1):
                arrive(zz, lane_y)
                start(push(zz, lane_y, me_c, ag_yc))
        if s >= 2:
            for zz in slices(s - 2):
                arrive(zz, lane_c)
                arrive(zz, lane_d)
                project(zz)

    kvw[1] = acc[...].astype(BF16)
    to_right = remote(kvw.at[1], kvw.at[0], halo_snd.at[0], halo_rcv.at[0], right)
    to_left = remote(kvw.at[1], kvw.at[2], halo_snd.at[1], halo_rcv.at[1], left)
    start(to_right)
    start(to_left)
    if n_pipe > 1:
        shift = remote(up_ref, up_v, up_snd, up_rcv, ctx, pipe_prev)
        start(shift)
    else:
        shift = pltpu.make_async_copy(up_ref, up_v, up_rcv)
        shift.start()
    loads[2].wait()
    loads[3].wait()
    to_right.wait_recv()
    to_left.wait_recv()

    key_pos = lax.broadcasted_iota(jnp.int32, (rows, rows), 0)
    query_pos = lax.broadcasted_iota(jnp.int32, (rows, rows), 1)
    lower = key_pos >= query_pos
    upper = key_pos <= query_pos

    def attention(group, first, last):
        def pair(i, carry):
            keys = kvw[:, :, group * HEAD_DIM:(group + 1) * HEAD_DIM].reshape(3 * rows, HEAD_DIM)
            at_v = (KV_HEADS + group) * HEAD_DIM
            values = kvw[:, :, at_v:at_v + HEAD_DIM].reshape(3 * rows, HEAD_DIM)
            made = []
            for j in range(2):
                at = pl.multiple_of((group * PER_GROUP + 2 * i + j) * HEAD_DIM, HEAD_DIM)
                query = q_v[:, pl.ds(at, HEAD_DIM)]
                grad = g_v[:, pl.ds(at, HEAD_DIM)]
                scores = dot(keys, query, NT) * scale
                scores = jnp.concatenate(
                    [
                        jnp.where(lower, scores[:rows], -1e30),
                        scores[rows:2 * rows],
                        jnp.where(upper, scores[2 * rows:], -1e30),
                    ],
                    axis=0,
                )
                peak = jnp.max(scores, axis=0, keepdims=True)
                lifted = jnp.exp(scores - peak)
                probs = lifted * (1.0 / jnp.sum(lifted, axis=0, keepdims=True))
                d_probs = dot(values, grad, NT)
                row_dot = jnp.sum(probs * d_probs, axis=0, keepdims=True)
                d_scores = (probs * (d_probs - row_dot) * scale).astype(BF16)
                d_query = dot(d_scores, keys, (((0,), (0,)), ((), ())))
                dq_v[:, pl.ds(at, HEAD_DIM)] = d_query.astype(BF16)
                made.append((d_scores, probs.astype(BF16), query, grad))
            d_keys = dot(
                jnp.concatenate([made[0][0], made[1][0]], axis=1),
                jnp.concatenate([made[0][2], made[1][2]], axis=0),
            )
            d_values = dot(
                jnp.concatenate([made[0][1], made[1][1]], axis=1),
                jnp.concatenate([made[0][3], made[1][3]], axis=0),
            )
            dkw[group, :, :HEAD_DIM] += d_keys
            dkw[group, :, HEAD_DIM:] += d_values
            return carry

        lax.fori_loop(first, last, pair, 0)

    def fold_copies(group):
        return (
            remote(dkw.at[group, pl.ds(2 * rows, rows)], fold.at[0, group],
                   fold_snd.at[0, group], fold_rcv.at[0, group], right),
            remote(dkw.at[group, pl.ds(0, rows)], fold.at[1, group],
                   fold_snd.at[1, group], fold_rcv.at[1, group], left),
        )

    def fold_start(group):
        for copy in fold_copies(group):
            start(copy)

    def share_start(group):
        for copy in fold_copies(group):
            copy.wait_recv()
        total = dkw[group, rows:2 * rows] + fold[0, group] + fold[1, group]
        high = total.astype(BF16)
        low = (total - high.astype(F32)).astype(BF16)
        dkv_sh[lane, group] = high
        at_k, at_v = group * HEAD_DIM, (KV_HEADS + group) * HEAD_DIM
        for into, part in ((dkv_hi, high), (dkv_lo, low)):
            into[:, at_k:at_k + HEAD_DIM] = part[:, :HEAD_DIM]
            into[:, at_v:at_v + HEAD_DIM] = part[:, HEAD_DIM:]
        own = dkv_sh.at[lane, group]
        start(remote(own, own, sh_snd.at[0, group], sh_rcv.at[group, lane], me_y))
        start(remote(own, own, sh_snd.at[1, group], sh_rcv.at[group, lane], me_c))

    def shared(group, ll, snd):
        part = dkv_sh.at[ll, group]
        return remote(part, part, snd, sh_rcv.at[group, ll], me_c)

    def share_pass(group):
        passed = shared(group, lane_y, shf_snd.at[group])
        passed.wait_recv()
        start(passed)

    def ring_copy(group, step, plus):
        snd, rcv = (p_snd, p_rcv) if plus else (m_snd, m_rcv)
        s_sem, r_sem = (ps_snd, ps_rcv) if plus else (ms_snd, ms_rcv)
        return remote(
            snd.at[group, step - 1], rcv.at[group, step - 1],
            s_sem.at[group, step - 1], r_sem.at[group, step - 1],
            z_next if plus else z_prev,
        )

    def ring_start(group):
        for ll in (lane_c, lane_d):
            shared(group, ll, shf_snd.at[group]).wait_recv()
        held = jnp.concatenate(
            [nt_sh[p].reshape(zs * feats, rows) for p in range(LANES)], axis=1
        )
        terms = dot(held, dkv_sh[:, group].reshape(LANES * rows, 2 * HEAD_DIM))
        prod[group] = terms.reshape(zs, feats, 2 * HEAD_DIM)
        p_snd[group, 0] = prod[group, at_z(hp)]
        start(ring_copy(group, 1, True))
        if hm > 0:
            m_snd[group, 0] = prod[group, at_z(-hm)]
            start(ring_copy(group, 1, False))

    def ring_step(group, step):
        ring_copy(group, step, True).wait_recv()
        if step < hp:
            p_snd[group, step] = p_rcv[group, step - 1] + prod[group, at_z(hp - step)]
            start(ring_copy(group, step + 1, True))
        if step <= hm:
            ring_copy(group, step, False).wait_recv()
            if step < hm:
                m_snd[group, step] = m_rcv[group, step - 1] + prod[group, at_z(step - hm)]
                start(ring_copy(group, step + 1, False))
        if step == hp:
            total = prod[group, z] + p_rcv[group, hp - 1]
            if hm > 0:
                total = total + m_rcv[group, hm - 1]
            total = total * (1.0 / math.sqrt(rows * n_ctx))
            at_k, at_v = group * HEAD_DIM, (KV_HEADS + group) * HEAD_DIM
            wg_v[:, at_k:at_k + HEAD_DIM] = total[:, :HEAD_DIM]
            wg_v[:, at_v:at_v + HEAD_DIM] = total[:, HEAD_DIM:]

    pairs = PER_GROUP // 2
    dkw[...] = jnp.zeros_like(dkw)
    attention(0, 0, pairs)
    fold_start(0)
    attention(1, 0, pairs // 2)
    share_start(0)
    attention(1, pairs // 2, pairs)
    fold_start(1)
    store_q = pltpu.make_async_copy(dq_v, dq_ref, out_sem.at[0])
    store_q.start()
    share_pass(0)
    for ll, to in ((lane_c, me_c), (lane_y, me_y), (lane_d, me_d)):
        remote(nt_sh.at[ll], nt_sh.at[ll], nt_snd.at[0], nt_rcv.at[ll], to).wait_recv()
    ring_start(0)
    share_start(1)
    share_pass(1)
    ring_start(1)

    model = z_v.shape[1]
    blocks = 8
    span = model // blocks
    dot_sum[...] = jnp.zeros_like(dot_sum)

    def spread(b):
        w_b = w_v[b * span:(b + 1) * span, :]
        d_b = dot(dkv_hi[...], w_b, NT) + dot(dkv_lo[...], w_b, NT)
        dn[:, b * span:(b + 1) * span] = d_b
        normed = z_v[:, b * span:(b + 1) * span].astype(F32) * fac[:, :1]
        part = d_b * normed
        total = part[:, :128]
        for k in range(1, span // 128):
            total = total + part[:, k * 128:(k + 1) * 128]
        dot_sum[...] += total

    def finish(b, mean):
        at = slice(b * span, (b + 1) * span)
        normed = z_v[:, at].astype(F32) * fac[:, :1]
        branch = fac[:, :1] * (dn[:, at] - normed * mean)
        go_v[:, at] = (up_v[:, at].astype(F32) + branch).astype(BF16)

    todo = [functools.partial(spread, b) for b in range(blocks)]

    def last():
        if n_pipe > 1:
            shift.wait_recv()
        else:
            shift.wait()
        mean = jnp.sum(dot_sum[...], axis=-1, keepdims=True) * (1.0 / model)
        for b in range(blocks):
            finish(b, mean)
        pltpu.make_async_copy(go_v, go_ref, out_sem.at[1]).start()

    todo.append(last)
    each = -(-len(todo) // max(1, hp - 1))
    for step in range(1, hp + 1):
        for group in range(KV_HEADS):
            ring_step(group, step)
        for _ in range(each):
            if todo:
                todo.pop(0)()
    while todo:
        todo.pop(0)()

    store_w = pltpu.make_async_copy(wg_v, wg_ref, out_sem.at[2])
    store_w.start()
    for copy in pushes:
        copy.wait_send()
    store_q.wait()
    pltpu.make_async_copy(go_v, go_ref, out_sem.at[1]).wait()
    store_w.wait()


def per_device(n_pipe, n_ctx, saved_in, grad_in, queries, d_heads, kv_weights):
    rows, model = saved_in.shape[1:]
    feats, kv_all = kv_weights.shape[1:]
    zs = n_ctx // LANES
    hp = zs // 2
    hm = max(1, zs - 1 - hp)
    pair = 2 * HEAD_DIM
    vm = pltpu.VMEM
    dma = pltpu.SemaphoreType.DMA
    big = vm((rows, model), BF16)
    scratch = [
        big, big, big, big, big, big, vm((feats, kv_all), F32),
        big, vm((rows, 128), F32),
        vm((zs, LANES, feats, rows), BF16), vm((LANES, zs, feats, rows), BF16),
        vm((n_ctx * feats, kv_all), BF16), vm((3, rows, kv_all), BF16), vm((rows, kv_all), F32),
        vm((KV_HEADS, 3 * rows, pair), F32), vm((2, KV_HEADS, rows, pair), F32),
        vm((rows, kv_all), BF16), vm((rows, kv_all), BF16),
        vm((LANES, KV_HEADS, rows, pair), BF16), vm((KV_HEADS, zs, feats, pair), F32),
        vm((rows, model), F32), vm((rows, 128), F32),
        vm((KV_HEADS, hp, feats, pair), F32), vm((KV_HEADS, hp, feats, pair), F32),
        vm((KV_HEADS, hm, feats, pair), F32), vm((KV_HEADS, hm, feats, pair), F32),
        dma((4,)), dma((3,)),
        dma((n_ctx,)), dma((zs,)), dma((zs,)), dma((zs,)), dma((zs,)), dma((zs,)),
        dma((3,)), dma((LANES,)), dma, dma,
        dma((2,)), dma((2,)), dma((2, KV_HEADS)), dma((2, KV_HEADS)),
        dma((2, KV_HEADS)), dma((KV_HEADS, LANES)), dma((KV_HEADS,)),
        dma((KV_HEADS, hp)), dma((KV_HEADS, hp)), dma((KV_HEADS, hm)), dma((KV_HEADS, hm)),
    ]
    any_space = pl.BlockSpec(memory_space=pl.ANY)
    grad_out, d_queries, weight_grad = pl.pallas_call(
        functools.partial(kernel, n_pipe, n_ctx),
        out_shape=(
            jax.ShapeDtypeStruct((rows, model), BF16),
            jax.ShapeDtypeStruct((rows, model), BF16),
            jax.ShapeDtypeStruct((feats, kv_all), F32),
        ),
        in_specs=[any_space] * 5,
        out_specs=(any_space,) * 3,
        scratch_shapes=scratch,
        compiler_params=pltpu.CompilerParams(
            collective_id=0, has_side_effects=True, vmem_limit_bytes=48 * 1024 * 1024
        ),
        name="step",
    )(saved_in[0], grad_in[0], queries[0], d_heads[0], kv_weights[0])
    return grad_out[None], d_queries[None], weight_grad[None]


def solution(mesh):
    spec = P("pipe", "ctx", None)
    return jax.shard_map(
        functools.partial(per_device, mesh.shape["pipe"], mesh.shape["ctx"]),
        mesh=mesh, in_specs=(spec,) * 5, out_specs=(spec,) * 3, check_vma=False,
    )
```

time: 421 us -> 114 us (0.27)
  the two profiles are of different devices: /device:TPU:1 before, /device:TPU:6 now
where the time goes in v1:
time: 114 us; the launch traced here: 113 us
  Pallas kernels  106 us (93%)
  local copies, waits for them, and re-layouts  7.13 us (6%)
    pallas_call x1, Pallas kernels, per_device(): pl.pallas_call(functools.partial(kernel, n_pipe, n_ctx), out_shape=(jax.S...  106 us
    unnamed x13, local copies, waits for them, and re-layouts  7.13 us

profile of v1, /device:TPU:6, one launch (start us, length us, event | category | flops | bytes accessed | tf_op | source)
XLA Modules:
  0.0 113.4 jit_solution(5892210373555452711)
XLA Ops:
  0.6 0.0 copy-start
  0.6 1.0 copy-done
  1.7 0.0 copy-start.1
  1.7 1.0 copy-done.1
  2.7 0.0 copy-start.2
  2.7 1.0 copy-done.2
  3.8 0.0 copy-start.3
  3.8 1.0 copy-done.3
  4.8 0.0 copy-start.4
  4.8 0.8 copy-done.4
  5.6 105.6 %step.1 = (bf16[128,2048]{1,0:T(8,128)(2,1)S(1)}, bf16[128,2048]{1,0:T(8,128)(2,1)S(1)}, f32[32,512]{1,0:T(8,128)S(1)}) custom-call(bf16[128,2048]{1,0:T(8,128)(2,1)S(1)} %bitcast.10, bf16[128,2048]{1,0:T(8,128)(2,1)S(1)} %bitcast.11, bf16[128,2048]{1,0:T(8,128)(2,1)S(1)} %bitcast.12, bf16[128,2048]{1,0:T(8,128)(2,1)S(1)} %bitcast.13, ...), custom_call_target="tpu_custom_call" | custom-call | tf_op jit(solution)/shard_map/step/pallas_call | solution.py:414
  111.2 0.8 copy.11
  112.0 0.8 copy.12
  112.8 0.6 copy.13
Async XLA Ops:
  0.6 1.0 copy-start
  1.7 1.0 copy-start.1
  2.7 1.0 copy-start.2
  3.8 1.0 copy-start.3
  4.8 0.8 copy-start.4

commit v2 on v1

v2 whole, which is shorter than its diff:
```python
import functools
import math

import jax
import jax.numpy as jnp
from jax import lax
from jax.experimental import pallas as pl
from jax.experimental.pallas import tpu as pltpu
from jax.sharding import PartitionSpec as P

HEADS = 16
HEAD_DIM = 128
KV_HEADS = 2
PER_GROUP = HEADS // KV_HEADS
LANES = 4
REACH = 4
EPSILON = 1e-06

F32 = jnp.float32
BF16 = jnp.bfloat16
NT = (((1,), (1,)), ((), ()))


def dot(a, b, dims=(((1,), (0,)), ((), ()))):
    return lax.dot_general(a, b, dims, preferred_element_type=F32)


def kernel(
    n_pipe, n_ctx,
    z_ref, up_ref, q_ref, g_ref, w_ref,
    go_v, dq_v, wg_v,
    z_v, q_v, g_v, up_v,
    nb, fac, nt, nt_sh, w_v, kvw, acc,
    dkw, fold, dkv_hi, dkv_lo, dkv_sh, prod, dn, dot_sum,
    p_snd, p_rcv, m_snd, m_rcv,
    loc_sem, ag_snd, ag_z, ag_y, ag_c,
    nt_snd, nt_rcv, up_snd, up_rcv,
    halo_snd, halo_rcv, fold_snd, fold_rcv,
    sh_snd, sh_rcv,
    p_sent, p_came, m_sent, m_came,
):
    rows = z_v.shape[0]
    zs = n_ctx // LANES
    hp = zs // 2
    hm = zs - 1 - hp
    feats = w_ref.shape[0]
    width = LANES * feats
    scale = 1.0 / math.sqrt(HEAD_DIM)

    pipe = lax.axis_index("pipe")
    ctx = lax.axis_index("ctx")
    z = ctx // LANES
    lane = lax.rem(ctx, LANES)
    y = lane // 2
    core = lax.rem(lane, 2)
    lane_c = 2 * y + (1 - core)
    lane_y = 2 * (1 - y) + core
    lane_d = 2 * (1 - y) + (1 - core)

    def at_z(distance):
        return lax.rem(z + distance + zs, zs)

    def dev(zz, ll):
        return zz * LANES + ll

    ups = [dev(at_z(k), lane) for k in range(1, min(max(2, REACH), hp) + 1)]
    downs = [dev(at_z(-k), lane) for k in range(1, min(max(2, REACH), hp) + 1)]
    me_c, me_y, me_d = dev(z, lane_c), dev(z, lane_y), dev(z, lane_d)
    right = lax.rem(ctx + 1, n_ctx)
    left = lax.rem(ctx + n_ctx - 1, n_ctx)
    pipe_prev = lax.rem(pipe + n_pipe - 1, n_pipe)
    pipe_next = lax.rem(pipe + 1, n_pipe)

    def remote(src, dst, snd, rcv, to, to_pipe=None):
        return pltpu.make_async_remote_copy(
            src_ref=src, dst_ref=dst, send_sem=snd, recv_sem=rcv,
            device_id=(pipe if to_pipe is None else to_pipe, to),
            device_id_type=pl.DeviceIdType.MESH,
        )

    loads = [
        pltpu.make_async_copy(z_ref, z_v, loc_sem.at[0]),
        pltpu.make_async_copy(
            w_ref, w_v.at[pl.ds(pl.multiple_of(ctx * feats, feats), feats)], loc_sem.at[1]
        ),
        pltpu.make_async_copy(q_ref, q_v, loc_sem.at[2]),
        pltpu.make_async_copy(g_ref, g_v, loc_sem.at[3]),
    ]
    for load in loads:
        load.start()

    with jax.named_scope("greet"):
        barrier = pltpu.get_barrier_semaphore()
        greeted = [(pipe, d) for d in (*ups, *downs, me_c, me_y, me_d, right, left)]
        if n_pipe > 1:
            greeted += [(pipe_prev, ctx), (pipe_next, ctx)]
        for who in greeted:
            pl.semaphore_signal(barrier, inc=1, device_id=who, device_id_type=pl.DeviceIdType.MESH)
        pl.semaphore_wait(barrier, len(greeted))

    def piece_at(zz, ll):
        return w_v.at[pl.ds(pl.multiple_of((zz * LANES + ll) * feats, feats), feats)]

    def pieces(count):
        return w_v.at[pl.ds(0, count * feats)]

    sent = [0]

    def push(zz, ll, to, came, own=False):
        sent[0] += 1
        remote(w_ref if own else piece_at(zz, ll), piece_at(zz, ll), ag_snd, came, to).start()

    def arrive(count, came):
        remote(pieces(count), pieces(count), ag_snd, came, me_c).wait_recv()

    early = rows // 2

    def shift(part):
        at = pl.ds(0, early) if part == 0 else pl.ds(early, rows - early)
        if n_pipe > 1:
            return remote(up_ref.at[at], up_v.at[at], up_snd, up_rcv, ctx, pipe_prev)
        return pltpu.make_async_copy(up_ref.at[at], up_v.at[at], up_rcv)

    def chain(distance, upward):
        reach, to = (hp, ups) if upward else (hm, downs)
        zz = at_z(-distance if upward else distance)
        for stride in (1, 2) if distance == 0 else (2,):
            if distance + stride <= reach:
                push(zz, lane, to[stride - 1], ag_z.at[int(upward), distance + stride - 1], own=distance == 0)

    chain(0, True)
    chain(0, False)
    push(z, lane, me_y, ag_y.at[0], own=True)
    push(z, lane, me_c, ag_c.at[0], own=True)

    with jax.named_scope("norm"):
        loads[0].wait()
        z_wide = z_v[...].astype(F32)
        factor = lax.rsqrt(jnp.mean(z_wide * z_wide, axis=-1, keepdims=True) + EPSILON)
        fac[...] = jnp.broadcast_to(factor, fac.shape)
        nb[...] = (z_wide * factor).astype(BF16)
        for k in range(zs):
            block = nb[:, k * width:(k + 1) * width].astype(F32)
            nt[k] = block.T.astype(BF16).reshape(LANES, feats, rows)

    shift(0).start()
    nt_sh[lane] = nt[:, lane]
    loads[1].wait()
    acc[...] = jnp.zeros_like(acc)

    def project(zz):
        at = pl.multiple_of(zz * width, width)
        acc[...] += dot(nb[:, pl.ds(at, width)], w_v[pl.ds(at, width), :])

    def slices(s):
        if s == 0:
            return [z]
        return ([at_z(-s)] if s <= hp else []) + ([at_z(s)] if s <= hm else [])

    y_lag, c_lag = 3, 5

    def cross(s):
        found = slices(s)
        arrive(len(found), ag_y.at[s])
        for zz in found:
            push(zz, lane_y, me_c, ag_c.at[s])

    for s in range(1, hp + c_lag + 1):
        with jax.named_scope(f"ag{s}"):
            if s <= hp:
                for zz, upward in zip(slices(s), (True, False)):
                    arrive(1, ag_z.at[int(upward), s - 1])
                    chain(s, upward)
                    push(zz, lane, me_y, ag_y.at[s])
                    push(zz, lane, me_c, ag_c.at[s])
                for back in range(max(0, s - y_lag), hp + 1) if s == hp else [s - y_lag]:
                    if back >= 0:
                        cross(back)
            if s >= c_lag:
                found = slices(s - c_lag)
                arrive(2 * len(found), ag_c.at[s - c_lag])
                for zz in found:
                    project(zz)

    def halo_copies(group):
        own = kvw.at[group, 1]
        return (
            remote(own, kvw.at[group, 0], halo_snd, halo_rcv.at[group], right),
            remote(own, kvw.at[group, 2], halo_snd, halo_rcv.at[group], left),
        )

    for group in range(KV_HEADS):
        at_k, at_v = group * HEAD_DIM, (KV_HEADS + group) * HEAD_DIM
        kvw[group, 1, 0] = acc[:, at_k:at_k + HEAD_DIM].astype(BF16)
        kvw[group, 1, 1] = acc[:, at_v:at_v + HEAD_DIM].astype(BF16)
        for copy in halo_copies(group):
            copy.start()
    loads[2].wait()
    loads[3].wait()

    def halo_wait(group):
        both = kvw.at[group, pl.ds(0, 2)]
        remote(both, both, halo_snd, halo_rcv.at[group], right).wait_recv()

    key_pos = lax.broadcasted_iota(jnp.int32, (rows, rows), 0)
    query_pos = lax.broadcasted_iota(jnp.int32, (rows, rows), 1)
    lower = key_pos >= query_pos
    upper = key_pos <= query_pos

    def attention(group, first, count, batch):
        def some(i, carry):
            keys = kvw[group, :, 0].reshape(3 * rows, HEAD_DIM)
            values = kvw[group, :, 1].reshape(3 * rows, HEAD_DIM)
            made = []
            for j in range(batch):
                head = group * PER_GROUP + first + batch * i + j
                at = pl.multiple_of(head * HEAD_DIM, HEAD_DIM)
                query = q_v[:, pl.ds(at, HEAD_DIM)]
                grad = g_v[:, pl.ds(at, HEAD_DIM)]
                scores = dot(keys, query, NT) * scale
                scores = jnp.concatenate(
                    [
                        jnp.where(lower, scores[:rows], -1e30),
                        scores[rows:2 * rows],
                        jnp.where(upper, scores[2 * rows:], -1e30),
                    ],
                    axis=0,
                )
                peak = jnp.max(scores, axis=0, keepdims=True)
                lifted = jnp.exp(scores - peak)
                probs = lifted * (1.0 / jnp.sum(lifted, axis=0, keepdims=True))
                d_probs = dot(values, grad, NT)
                row_dot = jnp.sum(probs * d_probs, axis=0, keepdims=True)
                d_scores = (probs * (d_probs - row_dot) * scale).astype(BF16)
                d_query = dot(d_scores, keys, (((0,), (0,)), ((), ())))
                dq_v[:, pl.ds(at, HEAD_DIM)] = d_query.astype(BF16)
                made.append((d_scores, probs.astype(BF16), query, grad))
            d_scores, probs, query, grad = (tuple(m[k] for m in made) for k in range(4))
            d_keys = dot(jnp.concatenate(d_scores, axis=1), jnp.concatenate(query, axis=0))
            d_values = dot(jnp.concatenate(probs, axis=1), jnp.concatenate(grad, axis=0))
            dkw[group, :, :HEAD_DIM] += d_keys
            dkw[group, :, HEAD_DIM:] += d_values
            return carry

        lax.fori_loop(0, count // batch, some, 0)

    def fold_start(group):
        for side, start, to in ((0, 2 * rows, right), (1, 0, left)):
            remote(
                dkw.at[group, pl.ds(start, rows)], fold.at[group, side], fold_snd, fold_rcv.at[group], to
            ).start()

    def share_start(group):
        remote(fold.at[group], fold.at[group], fold_snd, fold_rcv.at[group], right).wait_recv()
        total = dkw[group, rows:2 * rows] + fold[group, 0] + fold[group, 1]
        high = total.astype(BF16)
        low = (total - high.astype(F32)).astype(BF16)
        dkv_sh[lane, group] = high
        at_k, at_v = group * HEAD_DIM, (KV_HEADS + group) * HEAD_DIM
        for into, part in ((dkv_hi, high), (dkv_lo, low)):
            into[:, at_k:at_k + HEAD_DIM] = part[:, :HEAD_DIM]
            into[:, at_v:at_v + HEAD_DIM] = part[:, HEAD_DIM:]
        share(group, lane, 0, me_y).start()
        share(group, lane, 1, me_c).start()

    def share(group, ll, kind, to):
        part = dkv_sh.at[ll, group]
        return remote(part, part, sh_snd, sh_rcv.at[group, kind], to)

    def share_pass(group):
        share(group, lane_y, 0, me_c).wait_recv()
        share(group, lane_y, 1, me_c).start()

    def ring_refs(upward):
        if upward:
            return p_snd, p_rcv, p_sent, p_came, ups, hp
        return m_snd, m_rcv, m_sent, m_came, downs, hm

    def ring_send(group, k, upward, total):
        snd, rcv, s_sem, r_sem, to, _ = ring_refs(upward)
        far = int(k > REACH)
        snd[group, k - 1] = total.astype(BF16)
        remote(
            snd.at[group, k - 1], rcv.at[group, k - 1], s_sem, r_sem.at[group, far],
            to[(k - REACH if far else k) - 1],
        ).start()

    def ring_wait(group, upward, first, count, far):
        _, rcv, s_sem, r_sem, to, _ = ring_refs(upward)
        some = rcv.at[group, pl.ds(first, count)]
        remote(some, some, s_sem, r_sem.at[group, far], to[0]).wait_recv()
        return [rcv[group, first + k].astype(F32) for k in range(count)]

    def ring_start(group):
        two = dkv_sh.at[pl.ds(0, 2), group]
        remote(two, two, sh_snd, sh_rcv.at[group, 1], me_c).wait_recv()
        held = jnp.concatenate(
            [nt_sh[p].reshape(zs * feats, rows) for p in range(LANES)], axis=1
        )
        terms = dot(held, dkv_sh[:, group].reshape(LANES * rows, 2 * HEAD_DIM))
        prod[group] = terms.reshape(zs, feats, 2 * HEAD_DIM)
        for k in range(hp, 0, -1):
            for upward, reach in ((True, hp), (False, hm)):
                if k <= reach and (k != REACH or reach <= REACH):
                    ring_send(group, k, upward, prod[group, at_z(k if upward else -k)])

    def ring_middle(group):
        for upward, reach in ((True, hp), (False, hm)):
            if reach > REACH:
                total = prod[group, at_z(REACH if upward else -REACH)]
                for term in ring_wait(group, upward, REACH, reach - REACH, 1):
                    total = total + term
                ring_send(group, REACH, upward, total)

    def ring_end(group):
        total = prod[group, z]
        for upward, reach in ((True, hp), (False, hm)):
            if reach > 0:
                for term in ring_wait(group, upward, 0, min(REACH, reach), 0):
                    total = total + term
        total = total * (1.0 / math.sqrt(rows * n_ctx))
        at_k, at_v = group * HEAD_DIM, (KV_HEADS + group) * HEAD_DIM
        wg_v[:, at_k:at_k + HEAD_DIM] = total[:, :HEAD_DIM]
        wg_v[:, at_v:at_v + HEAD_DIM] = total[:, HEAD_DIM:]

    dkw[...] = jnp.zeros_like(dkw)
    with jax.named_scope("halo0"):
        halo_wait(0)
    for ll, to in ((lane_c, me_c), (lane_y, me_y), (lane_d, me_d)):
        remote(nt.at[:, ll], nt_sh.at[lane], nt_snd, nt_rcv, to).start()
    with jax.named_scope("att0"):
        attention(0, 0, PER_GROUP, 4)
    fold_start(0)
    with jax.named_scope("halo1"):
        halo_wait(1)
    with jax.named_scope("att1a"):
        attention(1, 0, 4, 4)
        attention(1, 4, 2, 2)
    with jax.named_scope("share0"):
        share_start(0)
    with jax.named_scope("att1b"):
        attention(1, 6, 2, 2)
    fold_start(1)
    with jax.named_scope("nt"):
        three = nt_sh.at[pl.ds(0, LANES - 1)]
        remote(three, three, nt_snd, nt_rcv, me_c).wait_recv()
    with jax.named_scope("pass0"):
        share_pass(0)
    with jax.named_scope("ring0"):
        ring_start(0)
    with jax.named_scope("share1"):
        share_start(1)

    model = z_v.shape[1]
    blocks = 8
    span = model // blocks
    dot_sum[...] = jnp.zeros_like(dot_sum)

    def spread(b):
        w_b = w_v[b * span:(b + 1) * span, :]
        d_b = dot(dkv_hi[...], w_b, NT) + dot(dkv_lo[...], w_b, NT)
        dn[:, b * span:(b + 1) * span] = d_b
        normed = z_v[:, b * span:(b + 1) * span].astype(F32) * fac[:, :1]
        part = d_b * normed
        total = part[:, :128]
        for k in range(1, span // 128):
            total = total + part[:, k * 128:(k + 1) * 128]
        dot_sum[...] += total

    def finish(b, mean):
        at = slice(b * span, (b + 1) * span)
        normed = z_v[:, at].astype(F32) * fac[:, :1]
        branch = fac[:, :1] * (dn[:, at] - normed * mean)
        go_v[:, at] = (up_v[:, at].astype(F32) + branch).astype(BF16)

    todo = [functools.partial(spread, b) for b in range(blocks)]

    def last():
        with jax.named_scope("up"):
            if n_pipe > 1:
                remote(up_v, up_v, up_snd, up_rcv, ctx, pipe_prev).wait_recv()
            else:
                pltpu.make_async_copy(up_ref, up_v, up_rcv).wait()
        mean = jnp.sum(dot_sum[...], axis=-1, keepdims=True) * (1.0 / model)
        for b in range(blocks):
            finish(b, mean)

    todo.append(last)
    def fill(count):
        for _ in range(count):
            if todo:
                todo.pop(0)()

    def stage(name, act):
        with jax.named_scope(name):
            act()

    stage("fill0", lambda: fill(4))
    stage("pass1", lambda: share_pass(1))
    stage("ring1", lambda: ring_start(1))
    stage("fill1", lambda: fill(1))
    stage("mid0", lambda: ring_middle(0))
    stage("fill2", lambda: fill(3))
    shift(1).start()
    stage("mid1", lambda: ring_middle(1))
    stage("end0", lambda: ring_end(0))
    stage("last", lambda: fill(len(todo)))
    stage("end1", lambda: ring_end(1))

    with jax.named_scope("drain"):
        all_sent = [
            (pieces(sent[0]), ag_snd), (nt.at[:, pl.ds(0, LANES - 1)], nt_snd),
            (kvw.at[:, pl.ds(0, 2)], halo_snd), (fold, fold_snd),
            (dkv_sh.at[pl.ds(0, LANES - 1)], sh_snd), (p_snd, p_sent),
        ]
        if hm > 0:
            all_sent.append((m_snd, m_sent))
        if n_pipe > 1:
            all_sent.append((up_v, up_snd))
        for ref, sem in all_sent:
            remote(ref, ref, sem, sem, me_c).wait_send()


def store(go_v, dq_v, wg_v, go_ref, dq_ref, wg_ref, sem):
    copies = [
        pltpu.make_async_copy(src, dst, sem.at[i])
        for i, (src, dst) in enumerate(((go_v, go_ref), (dq_v, dq_ref), (wg_v, wg_ref)))
    ]
    for copy in copies:
        copy.start()
    for copy in copies:
        copy.wait()


def per_device(n_pipe, n_ctx, saved_in, grad_in, queries, d_heads, kv_weights):
    rows, model = saved_in.shape[1:]
    feats, kv_all = kv_weights.shape[1:]
    zs = n_ctx // LANES
    hp = zs // 2
    hm = max(1, zs - 1 - hp)
    pair = 2 * HEAD_DIM
    vm = pltpu.VMEM
    dma = pltpu.SemaphoreType.DMA
    big = vm((rows, model), BF16)
    scratch = [
        big, big, big, big,
        big, vm((rows, 128), F32),
        vm((zs, LANES, feats, rows), BF16), vm((LANES, zs, feats, rows), BF16),
        vm((n_ctx * feats, kv_all), BF16), vm((KV_HEADS, 3, 2, rows, HEAD_DIM), BF16), vm((rows, kv_all), F32),
        vm((KV_HEADS, 3 * rows, pair), F32), vm((KV_HEADS, 2, rows, pair), F32),
        vm((rows, kv_all), BF16), vm((rows, kv_all), BF16),
        vm((LANES, KV_HEADS, rows, pair), BF16), vm((KV_HEADS, zs, feats, pair), F32),
        vm((rows, model), F32), vm((rows, 128), F32),
        vm((KV_HEADS, hp, feats, pair), BF16), vm((KV_HEADS, hp, feats, pair), BF16),
        vm((KV_HEADS, hm, feats, pair), BF16), vm((KV_HEADS, hm, feats, pair), BF16),
        dma((4,)), dma, dma((2, hp)), dma((hp + 1,)), dma((hp + 1,)),
        dma, dma, dma, dma,
        dma, dma((KV_HEADS,)), dma, dma((KV_HEADS,)),
        dma, dma((KV_HEADS, 2)),
        dma, dma((KV_HEADS, 2)), dma, dma((KV_HEADS, 2)),
    ]
    hbm = pl.BlockSpec(memory_space=pltpu.HBM)
    vmem = pl.BlockSpec(memory_space=pltpu.VMEM)
    shapes = (
        jax.ShapeDtypeStruct((rows, model), BF16),
        jax.ShapeDtypeStruct((rows, model), BF16),
        jax.ShapeDtypeStruct((feats, kv_all), F32),
    )
    results = pl.pallas_call(
        functools.partial(kernel, n_pipe, n_ctx),
        out_shape=shapes,
        in_specs=[hbm] * 5,
        out_specs=(vmem,) * 3,
        scratch_shapes=scratch,
        compiler_params=pltpu.CompilerParams(
            collective_id=0, has_side_effects=True, vmem_limit_bytes=48 * 1024 * 1024
        ),
        name="step",
    )(*(
        pltpu.with_memory_space_constraint(x[0], pltpu.HBM)
        for x in (saved_in, grad_in, queries, d_heads, kv_weights)
    ))
    grad_out, d_queries, weight_grad = pl.pallas_call(
        store,
        out_shape=shapes,
        in_specs=[vmem] * 3,
        out_specs=(hbm,) * 3,
        scratch_shapes=[dma((3,))],
        name="store",
    )(*(pltpu.with_memory_space_constraint(x, pltpu.VMEM) for x in results))
    return grad_out[None], d_queries[None], weight_grad[None]


def solution(mesh):
    spec = P("pipe", "ctx", None)
    return jax.shard_map(
        functools.partial(per_device, mesh.shape["pipe"], mesh.shape["ctx"]),
        mesh=mesh, in_specs=(spec,) * 5, out_specs=(spec,) * 3, check_vma=False,
    )
```

time: 114 us -> 74.1 us (0.65)
  the two profiles are of different devices: /device:TPU:6 before, /device:TPU:1 now
where the time goes in v2:
time: 74.1 us; the launch traced here: 74 us
  Pallas kernels  73.3 us (99%)
    pallas_call x1, Pallas kernels, per_device(): pl.pallas_call(functools.partial(kernel, n_pipe, n_ctx), out_shape=shapes...  72.3 us

profile of v2, /device:TPU:1, one launch (start us, length us, event | category | flops | bytes accessed | tf_op | source)
XLA Modules:
  0.0 74.0 jit_solution(8818788252454786860)
XLA Ops:
  0.6 72.3 %step.1 = (bf16[128,2048]{1,0:T(8,128)(2,1)S(1)}, bf16[128,2048]{1,0:T(8,128)(2,1)S(1)}, f32[32,512]{1,0:T(8,128)S(1)}) custom-call(bf16[128,2048]{1,0:T(8,128)(2,1)} %bitcast.8, bf16[128,2048]{1,0:T(8,128)(2,1)} %bitcast.9, bf16[128,2048]{1,0:T(8,128)(2,1)} %bitcast.10, bf16[128,2048]{1,0:T(8,128)(2,1)} %bitcast.11, bf16[32,512]{1,0:T(8,128)(2,1)} %bitcast.12), custom_call_target="tpu_custom_call" | custom-call | tf_op jit(solution)/shard_map/step/pallas_call | solution.py:469
  73.0 1.0 %store.1 = (bf16[128,2048]{1,0:T(8,128)(2,1)}, bf16[128,2048]{1,0:T(8,128)(2,1)}, f32[32,512]{1,0:T(8,128)}) custom-call(bf16[128,2048]{1,0:T(8,128)(2,1)S(1)} %get-tuple-element.9.go_v, bf16[128,2048]{1,0:T(8,128)(2,1)S(1)} %get-tuple-element.10.dq_v, f32[32,512]{1,0:T(8,128)S(1)} %get-tuple-element.11.wg_v), custom_call_target="tpu_custom_call" | custom-call | tf_op jit(solution)/shard_map/store/pallas_call | solution.py:483

commit v3 on v2

--- a/solution.py
+++ b/solution.py
@@ -25,16 +25,28 @@
     return lax.dot_general(a, b, dims, preferred_element_type=F32)
 
 
+def over_keys(op, last, a):
+    while a.shape[0] > 8:
+        parts = 3 if a.shape[0] % 3 == 0 else 2
+        step = a.shape[0] // parts
+        total = a[:step]
+        for k in range(1, parts):
+            total = op(total, a[k * step:(k + 1) * step])
+        a = total
+    return last(a, axis=0, keepdims=True)
+
+
 def kernel(
     n_pipe, n_ctx,
     z_ref, up_ref, q_ref, g_ref, w_ref,
     go_v, dq_v, wg_v,
-    z_v, q_v, g_v, up_v,
+    z_v, q_v, g_v, up_v, relay,
     nb, fac, nt, nt_sh, w_v, kvw, acc,
-    dkw, fold, dkv_hi, dkv_lo, dkv_sh, prod, dn, dot_sum,
+    dkw, folded, fold, dkv_hi, dkv_lo, dkv_sh, prod, dn, dot_sum,
     p_snd, p_rcv, m_snd, m_rcv,
+    s_buf, d_buf, p_all, d_all,
     loc_sem, ag_snd, ag_z, ag_y, ag_c,
-    nt_snd, nt_rcv, up_snd, up_rcv,
+    nt_snd, nt_rcv, up_snd, up_rcv, rl_snd, rl_rcv,
     halo_snd, halo_rcv, fold_snd, fold_rcv,
     sh_snd, sh_rcv,
     p_sent, p_came, m_sent, m_came,
@@ -63,18 +75,28 @@
     def dev(zz, ll):
         return zz * LANES + ll
 
-    ups = [dev(at_z(k), lane) for k in range(1, min(max(2, REACH), hp) + 1)]
-    downs = [dev(at_z(-k), lane) for k in range(1, min(max(2, REACH), hp) + 1)]
+    ups = [dev(at_z(k), lane) for k in range(1, min(max(4, REACH), hp) + 1)]
+    downs = [dev(at_z(-k), lane) for k in range(1, min(max(4, REACH), hp) + 1)]
     me_c, me_y, me_d = dev(z, lane_c), dev(z, lane_y), dev(z, lane_d)
     right = lax.rem(ctx + 1, n_ctx)
     left = lax.rem(ctx + n_ctx - 1, n_ctx)
-    pipe_prev = lax.rem(pipe + n_pipe - 1, n_pipe)
-    pipe_next = lax.rem(pipe + 1, n_pipe)
-
-    def remote(src, dst, snd, rcv, to, to_pipe=None):
+
+    xs = max(1, n_pipe // 2)
+    x, y_hi = pipe // 2, lax.rem(pipe, 2)
+    turn = 1 - 2 * core
+    y_on = lax.rem(2 * y_hi + y + turn + 4, 4)
+    y_back = lax.rem(2 * y_hi + y - turn + 4, 4)
+
+    def across(xx, yy):
+        return lax.rem(xx + xs, xs) * 2 + yy // 2, dev(z, 2 * lax.rem(yy, 2) + core)
+
+    relay_to, relay_from = across(x, y_on), across(x, y_back)
+    shift_to, shift_from = across(x - (1 - y_back // 2), y_on), across(x + y_hi, y_back)
+
+    def remote(src, dst, snd, rcv, to, where=None):
         return pltpu.make_async_remote_copy(
             src_ref=src, dst_ref=dst, send_sem=snd, recv_sem=rcv,
-            device_id=(pipe if to_pipe is None else to_pipe, to),
+            device_id=(pipe, to) if where is None else where,
             device_id_type=pl.DeviceIdType.MESH,
         )
 
@@ -93,7 +115,7 @@
         barrier = pltpu.get_barrier_semaphore()
         greeted = [(pipe, d) for d in (*ups, *downs, me_c, me_y, me_d, right, left)]
         if n_pipe > 1:
-            greeted += [(pipe_prev, ctx), (pipe_next, ctx)]
+            greeted += [relay_to, relay_from, shift_to, shift_from]
         for who in greeted:
             pl.semaphore_signal(barrier, inc=1, device_id=who, device_id_type=pl.DeviceIdType.MESH)
         pl.semaphore_wait(barrier, len(greeted))
@@ -113,18 +135,26 @@
     def arrive(count, came):
         remote(pieces(count), pieces(count), ag_snd, came, me_c).wait_recv()
 
-    early = rows // 2
-
-    def shift(part):
+    def shift(hop, part):
+        early = 3 * rows // 8
         at = pl.ds(0, early) if part == 0 else pl.ds(early, rows - early)
-        if n_pipe > 1:
-            return remote(up_ref.at[at], up_v.at[at], up_snd, up_rcv, ctx, pipe_prev)
-        return pltpu.make_async_copy(up_ref.at[at], up_v.at[at], up_rcv)
+        if hop == 0:
+            return remote(up_ref.at[at], relay.at[at], rl_snd, rl_rcv.at[part], None, relay_to)
+        return remote(relay.at[at], up_v.at[at], up_snd, up_rcv, None, shift_to)
+
+    def shift_start(hop, part):
+        if n_pipe == 1:
+            if (hop, part) == (0, 0):
+                pltpu.make_async_copy(up_ref, up_v, up_rcv).start()
+            return
+        if hop == 1:
+            shift(0, part).wait_recv()
+        shift(hop, part).start()
 
     def chain(distance, upward):
         reach, to = (hp, ups) if upward else (hm, downs)
         zz = at_z(-distance if upward else distance)
-        for stride in (1, 2) if distance == 0 else (2,):
+        for stride in (1, 2, 4) if distance % 4 == 0 else (1,) if distance % 2 == 0 else ():
             if distance + stride <= reach:
                 push(zz, lane, to[stride - 1], ag_z.at[int(upward), distance + stride - 1], own=distance == 0)
 
@@ -143,7 +173,12 @@
             block = nb[:, k * width:(k + 1) * width].astype(F32)
             nt[k] = block.T.astype(BF16).reshape(LANES, feats, rows)
 
-    shift(0).start()
+    def give(ll, to):
+        remote(nt.at[:, ll], nt_sh.at[lane], nt_snd, nt_rcv, to).start()
+    give(lane_d, me_d)
+    give(lane_y, me_y)
+    give(lane_c, me_c)
+    shift_start(0, 0)
     nt_sh[lane] = nt[:, lane]
     loads[1].wait()
     acc[...] = jnp.zeros_like(acc)
@@ -157,28 +192,38 @@
             return [z]
         return ([at_z(-s)] if s <= hp else []) + ([at_z(s)] if s <= hm else [])
 
-    y_lag, c_lag = 3, 5
+    order = [d for d in (1, 2, 4, 3, 5, 6, 8, 7) if d <= hp]
+    assert len(order) == hp
+    y_lag, c_lag = 4, 6
 
     def cross(s):
         found = slices(s)
+        if s == order[-1]:
+            arrive(2 * len(found), ag_y.at[s])
+            return
         arrive(len(found), ag_y.at[s])
         for zz in found:
             push(zz, lane_y, me_c, ag_c.at[s])
 
-    for s in range(1, hp + c_lag + 1):
-        with jax.named_scope(f"ag{s}"):
-            if s <= hp:
+    order = [0] + order
+    for i in range(1, hp + c_lag + 1):
+        with jax.named_scope(f"ag{i}"):
+            if i <= hp:
+                s = order[i]
                 for zz, upward in zip(slices(s), (True, False)):
                     arrive(1, ag_z.at[int(upward), s - 1])
                     chain(s, upward)
                     push(zz, lane, me_y, ag_y.at[s])
+                    if i == hp:
+                        push(zz, lane, me_d, ag_y.at[s])
                     push(zz, lane, me_c, ag_c.at[s])
-                for back in range(max(0, s - y_lag), hp + 1) if s == hp else [s - y_lag]:
+                for back in range(max(0, i - y_lag), hp + 1) if i == hp else [i - y_lag]:
                     if back >= 0:
-                        cross(back)
-            if s >= c_lag:
-                found = slices(s - c_lag)
-                arrive(2 * len(found), ag_c.at[s - c_lag])
+                        cross(order[back])
+            if i >= c_lag:
+                s = order[i - c_lag]
+                found = slices(s)
+                arrive((1 if s == order[-1] else 2) * len(found), ag_c.at[s])
                 for zz in found:
                     project(zz)
 
@@ -207,52 +252,78 @@
     lower = key_pos >= query_pos
     upper = key_pos <= query_pos
 
-    def attention(group, first, count, batch):
-        def some(i, carry):
-            keys = kvw[group, :, 0].reshape(3 * rows, HEAD_DIM)
-            values = kvw[group, :, 1].reshape(3 * rows, HEAD_DIM)
-            made = []
-            for j in range(batch):
-                head = group * PER_GROUP + first + batch * i + j
-                at = pl.multiple_of(head * HEAD_DIM, HEAD_DIM)
-                query = q_v[:, pl.ds(at, HEAD_DIM)]
-                grad = g_v[:, pl.ds(at, HEAD_DIM)]
-                scores = dot(keys, query, NT) * scale
-                scores = jnp.concatenate(
-                    [
-                        jnp.where(lower, scores[:rows], -1e30),
-                        scores[rows:2 * rows],
-                        jnp.where(upper, scores[2 * rows:], -1e30),
-                    ],
-                    axis=0,
-                )
-                peak = jnp.max(scores, axis=0, keepdims=True)
-                lifted = jnp.exp(scores - peak)
-                probs = lifted * (1.0 / jnp.sum(lifted, axis=0, keepdims=True))
-                d_probs = dot(values, grad, NT)
-                row_dot = jnp.sum(probs * d_probs, axis=0, keepdims=True)
-                d_scores = (probs * (d_probs - row_dot) * scale).astype(BF16)
-                d_query = dot(d_scores, keys, (((0,), (0,)), ((), ())))
-                dq_v[:, pl.ds(at, HEAD_DIM)] = d_query.astype(BF16)
-                made.append((d_scores, probs.astype(BF16), query, grad))
-            d_scores, probs, query, grad = (tuple(m[k] for m in made) for k in range(4))
-            d_keys = dot(jnp.concatenate(d_scores, axis=1), jnp.concatenate(query, axis=0))
-            d_values = dot(jnp.concatenate(probs, axis=1), jnp.concatenate(grad, axis=0))
-            dkw[group, :, :HEAD_DIM] += d_keys
-            dkw[group, :, HEAD_DIM:] += d_values
-            return carry
-
-        lax.fori_loop(0, count // batch, some, 0)
+    def attention(group, heads):
+        keys = kvw[group, :, 0].reshape(3 * rows, HEAD_DIM)
+        values = kvw[group, :, 1].reshape(3 * rows, HEAD_DIM)
+        parts = [slice(b * rows, (b + 1) * rows) for b in range(3)]
+
+        def lanes(h):
+            return slice((group * PER_GROUP + h) * HEAD_DIM, (group * PER_GROUP + h + 1) * HEAD_DIM)
+
+        def multiply(h):
+            slot = h % 2
+            scores = dot(keys, q_v[:, lanes(h)], NT)
+            s_buf[slot, parts[0]] = jnp.where(lower, scores[parts[0]], -1e30)
+            s_buf[slot, parts[1]] = scores[parts[1]]
+            s_buf[slot, parts[2]] = jnp.where(upper, scores[parts[2]], -1e30)
+            d_buf[slot] = dot(values, g_v[:, lanes(h)], NT)
+
+        def weigh(h):
+            slot, into = h % 2, slice(h * HEAD_DIM, (h + 1) * HEAD_DIM)
+            peak = jnp.maximum(jnp.maximum(s_buf[slot, parts[0]], s_buf[slot, parts[1]]), s_buf[slot, parts[2]])
+            peak = over_keys(jnp.maximum, jnp.max, peak)
+            total = row_dot = None
+            for part in parts:
+                lifted = jnp.exp2((s_buf[slot, part] - peak) * (scale * math.log2(math.e)))
+                s_buf[slot, part] = lifted
+                product = lifted * d_buf[slot, part]
+                total = lifted if total is None else total + lifted
+                row_dot = product if row_dot is None else row_dot + product
+            inverse = 1.0 / over_keys(jnp.add, jnp.sum, total)
+            row_dot = over_keys(jnp.add, jnp.sum, row_dot) * inverse
+            for part in parts:
+                lifted = s_buf[slot, part]
+                p_all[part, into] = (lifted * inverse).astype(BF16)
+                d_all[part, into] = (lifted * (inverse * scale) * (d_buf[slot, part] - row_dot)).astype(BF16)
+
+        def spread_query(h):
+            into = slice(h * HEAD_DIM, (h + 1) * HEAD_DIM)
+            d_query = dot(d_all[:, into], keys, (((0,), (0,)), ((), ())))
+            dq_v[:, lanes(h)] = d_query.astype(BF16)
+
+        def sum_heads(first, last):
+            into = slice(first * HEAD_DIM, last * HEAD_DIM)
+            for ref, source, at in ((d_all, q_v, 0), (p_all, g_v, HEAD_DIM)):
+                rest = jnp.concatenate([source[:, lanes(h)] for h in range(first, last)], axis=0)
+                total = dot(ref[:, into], rest)
+                if first > 0:
+                    total = total + dkw[group, :, at:at + HEAD_DIM]
+                dkw[group, :, at:at + HEAD_DIM] = total
+
+        half = PER_GROUP // 2
+        multiply(heads[0])
+        for h in heads:
+            if h != heads[-1]:
+                multiply(h + 1)
+            weigh(h)
+            if h != heads[0]:
+                spread_query(h - 1)
+            if h == half:
+                sum_heads(0, half)
+        spread_query(heads[-1])
+        if heads[-1] == PER_GROUP - 1:
+            sum_heads(half, PER_GROUP)
 
     def fold_start(group):
         for side, start, to in ((0, 2 * rows, right), (1, 0, left)):
+            folded[group, side] = dkw[group, start:start + rows].astype(BF16)
             remote(
-                dkw.at[group, pl.ds(start, rows)], fold.at[group, side], fold_snd, fold_rcv.at[group], to
+                folded.at[group, side], fold.at[group, side], fold_snd, fold_rcv.at[group], to
             ).start()
 
     def share_start(group):
         remote(fold.at[group], fold.at[group], fold_snd, fold_rcv.at[group], right).wait_recv()
-        total = dkw[group, rows:2 * rows] + fold[group, 0] + fold[group, 1]
+        total = dkw[group, rows:2 * rows] + fold[group, 0].astype(F32) + fold[group, 1].astype(F32)
         high = total.astype(BF16)
         low = (total - high.astype(F32)).astype(BF16)
         dkv_sh[lane, group] = high
@@ -260,8 +331,8 @@
         for into, part in ((dkv_hi, high), (dkv_lo, low)):
             into[:, at_k:at_k + HEAD_DIM] = part[:, :HEAD_DIM]
             into[:, at_v:at_v + HEAD_DIM] = part[:, HEAD_DIM:]
-        share(group, lane, 0, me_y).start()
-        share(group, lane, 1, me_c).start()
+        for kind, to in enumerate((me_y, me_c)):
+            share(group, lane, kind, to).start()
 
     def share(group, ll, kind, to):
         part = dkv_sh.at[ll, group]
@@ -323,33 +394,29 @@
         wg_v[:, at_k:at_k + HEAD_DIM] = total[:, :HEAD_DIM]
         wg_v[:, at_v:at_v + HEAD_DIM] = total[:, HEAD_DIM:]
 
-    dkw[...] = jnp.zeros_like(dkw)
     with jax.named_scope("halo0"):
         halo_wait(0)
-    for ll, to in ((lane_c, me_c), (lane_y, me_y), (lane_d, me_d)):
-        remote(nt.at[:, ll], nt_sh.at[lane], nt_snd, nt_rcv, to).start()
     with jax.named_scope("att0"):
-        attention(0, 0, PER_GROUP, 4)
+        attention(0, range(PER_GROUP))
     fold_start(0)
     with jax.named_scope("halo1"):
         halo_wait(1)
-    with jax.named_scope("att1a"):
-        attention(1, 0, 4, 4)
-        attention(1, 4, 2, 2)
+    with jax.named_scope("att1"):
+        attention(1, range(PER_GROUP))
+    fold_start(1)
     with jax.named_scope("share0"):
         share_start(0)
-    with jax.named_scope("att1b"):
-        attention(1, 6, 2, 2)
-    fold_start(1)
     with jax.named_scope("nt"):
         three = nt_sh.at[pl.ds(0, LANES - 1)]
         remote(three, three, nt_snd, nt_rcv, me_c).wait_recv()
     with jax.named_scope("pass0"):
         share_pass(0)
+    with jax.named_scope("share1"):
+        share_start(1)
+    shift_start(1, 0)
+    shift_start(0, 1)
     with jax.named_scope("ring0"):
         ring_start(0)
-    with jax.named_scope("share1"):
-        share_start(1)
 
     model = z_v.shape[1]
     blocks = 8
@@ -378,7 +445,7 @@
     def last():
         with jax.named_scope("up"):
             if n_pipe > 1:
-                remote(up_v, up_v, up_snd, up_rcv, ctx, pipe_prev).wait_recv()
+                remote(relay, up_v, up_snd, up_rcv, None, shift_to).wait_recv()
             else:
                 pltpu.make_async_copy(up_ref, up_v, up_rcv).wait()
         mean = jnp.sum(dot_sum[...], axis=-1, keepdims=True) * (1.0 / model)
@@ -395,13 +462,14 @@
         with jax.named_scope(name):
             act()
 
-    stage("fill0", lambda: fill(4))
+    stage("fill0", lambda: fill(3))
     stage("pass1", lambda: share_pass(1))
+    stage("fill1", lambda: fill(1))
     stage("ring1", lambda: ring_start(1))
-    stage("fill1", lambda: fill(1))
+    stage("fill1", lambda: fill(2))
     stage("mid0", lambda: ring_middle(0))
-    stage("fill2", lambda: fill(3))
-    shift(1).start()
+    stage("fwd", lambda: shift_start(1, 1))
+    stage("fill2", lambda: fill(2))
     stage("mid1", lambda: ring_middle(1))
     stage("end0", lambda: ring_end(0))
     stage("last", lambda: fill(len(todo)))
@@ -416,7 +484,7 @@
         if hm > 0:
             all_sent.append((m_snd, m_sent))
         if n_pipe > 1:
-            all_sent.append((up_v, up_snd))
+            all_sent += [(up_v, up_snd), (relay, rl_snd)]
         for ref, sem in all_sent:
             remote(ref, ref, sem, sem, me_c).wait_send()
 
@@ -443,18 +511,20 @@
     dma = pltpu.SemaphoreType.DMA
     big = vm((rows, model), BF16)
     scratch = [
-        big, big, big, big,
+        big, big, big, big, big,
         big, vm((rows, 128), F32),
         vm((zs, LANES, feats, rows), BF16), vm((LANES, zs, feats, rows), BF16),
         vm((n_ctx * feats, kv_all), BF16), vm((KV_HEADS, 3, 2, rows, HEAD_DIM), BF16), vm((rows, kv_all), F32),
-        vm((KV_HEADS, 3 * rows, pair), F32), vm((KV_HEADS, 2, rows, pair), F32),
+        vm((KV_HEADS, 3 * rows, pair), F32), vm((KV_HEADS, 2, rows, pair), BF16), vm((KV_HEADS, 2, rows, pair), BF16),
         vm((rows, kv_all), BF16), vm((rows, kv_all), BF16),
         vm((LANES, KV_HEADS, rows, pair), BF16), vm((KV_HEADS, zs, feats, pair), F32),
         vm((rows, model), F32), vm((rows, 128), F32),
         vm((KV_HEADS, hp, feats, pair), BF16), vm((KV_HEADS, hp, feats, pair), BF16),
         vm((KV_HEADS, hm, feats, pair), BF16), vm((KV_HEADS, hm, feats, pair), BF16),
+        vm((2, 3 * rows, HEAD_DIM), F32), vm((2, 3 * rows, HEAD_DIM), F32),
+        vm((3 * rows, PER_GROUP * HEAD_DIM), BF16), vm((3 * rows, PER_GROUP * HEAD_DIM), BF16),
         dma((4,)), dma, dma((2, hp)), dma((hp + 1,)), dma((hp + 1,)),
-        dma, dma, dma, dma,
+        dma, dma, dma, dma, dma, dma((2,)),
         dma, dma((KV_HEADS,)), dma, dma((KV_HEADS,)),
         dma, dma((KV_HEADS, 2)),
         dma, dma((KV_HEADS, 2)), dma, dma((KV_HEADS, 2)),

time: 74.1 us -> 70.6 us (0.953)
  Pallas kernels: 73.3 us -> 69.3 us
    pallas_call x1, Pallas kernels: 72.3 us -> 68.3 us  [per_device(): pl.pallas_call(functools.partial(kernel, n_pipe, n_ctx), out_shape=shapes...]
where the time goes in v3:
time: 70.6 us; the launch traced here: 69.9 us
  Pallas kernels  69.3 us (98%)
    pallas_call x1, Pallas kernels, per_device(): pl.pallas_call(functools.partial(kernel, n_pipe, n_ctx), out_shape=shapes...  68.3 us

profile of v3, /device:TPU:1, one launch (start us, length us, event | category | flops | bytes accessed | tf_op | source)
XLA Modules:
  0.0 69.9 jit_solution(241030199255208876)
XLA Ops:
  0.6 68.3 %step.1 = (bf16[128,2048]{1,0:T(8,128)(2,1)S(1)}, bf16[128,2048]{1,0:T(8,128)(2,1)S(1)}, f32[32,512]{1,0:T(8,128)S(1)}) custom-call(bf16[128,2048]{1,0:T(8,128)(2,1)} %bitcast.8, bf16[128,2048]{1,0:T(8,128)(2,1)} %bitcast.9, bf16[128,2048]{1,0:T(8,128)(2,1)} %bitcast.10, bf16[128,2048]{1,0:T(8,128)(2,1)} %bitcast.11, bf16[32,512]{1,0:T(8,128)(2,1)} %bitcast.12), custom_call_target="tpu_custom_call" | custom-call | tf_op jit(solution)/shard_map/step/pallas_call | solution.py:539
  68.9 1.0 %store.1 = (bf16[128,2048]{1,0:T(8,128)(2,1)}, bf16[128,2048]{1,0:T(8,128)(2,1)}, f32[32,512]{1,0:T(8,128)}) custom-call(bf16[128,2048]{1,0:T(8,128)(2,1)S(1)} %get-tuple-element.9.go_v, bf16[128,2048]{1,0:T(8,128)(2,1)S(1)} %get-tuple-element.10.dq_v, f32[32,512]{1,0:T(8,128)S(1)} %get-tuple-element.11.wg_v), custom_call_target="tpu_custom_call" | custom-call | tf_op jit(solution)/shard_map/store/pallas_call | solution.py:553

commit v4 on v3

--- a/solution.py
+++ b/solution.py
@@ -154,7 +154,8 @@
     def chain(distance, upward):
         reach, to = (hp, ups) if upward else (hm, downs)
         zz = at_z(-distance if upward else distance)
-        for stride in (1, 2, 4) if distance % 4 == 0 else (1,) if distance % 2 == 0 else ():
+        strides = {0: (1, 2, 4), 2: (1,), 4: (1, 2, 3, 4)}
+        for stride in strides.get(distance, ()):
             if distance + stride <= reach:
                 push(zz, lane, to[stride - 1], ag_z.at[int(upward), distance + stride - 1], own=distance == 0)
 
@@ -176,9 +177,7 @@
     def give(ll, to):
         remote(nt.at[:, ll], nt_sh.at[lane], nt_snd, nt_rcv, to).start()
     give(lane_d, me_d)
-    give(lane_y, me_y)
     give(lane_c, me_c)
-    shift_start(0, 0)
     nt_sh[lane] = nt[:, lane]
     loads[1].wait()
     acc[...] = jnp.zeros_like(acc)
@@ -192,9 +191,9 @@
             return [z]
         return ([at_z(-s)] if s <= hp else []) + ([at_z(s)] if s <= hm else [])
 
-    order = [d for d in (1, 2, 4, 3, 5, 6, 8, 7) if d <= hp]
+    order = [d for d in (1, 2, 4, 3, 5, 6, 7, 8) if d <= hp]
     assert len(order) == hp
-    y_lag, c_lag = 4, 6
+    y_lag, c_lag = 7, 8
 
     def cross(s):
         found = slices(s)
@@ -217,6 +216,9 @@
                     if i == hp:
                         push(zz, lane, me_d, ag_y.at[s])
                     push(zz, lane, me_c, ag_c.at[s])
+                if i == hp:
+                    give(lane_y, me_y)
+                    shift_start(0, 0)
                 for back in range(max(0, i - y_lag), hp + 1) if i == hp else [i - y_lag]:
                     if back >= 0:
                         cross(order[back])
@@ -347,19 +349,25 @@
             return p_snd, p_rcv, p_sent, p_came, ups, hp
         return m_snd, m_rcv, m_sent, m_came, downs, hm
 
+    def relayed(k):
+        return k == 3 and REACH > 3
+
+    def ring_slot(k):
+        return {3: 3, 4: 2}.get(k, k - 1) if REACH > 3 else k - 1
+
     def ring_send(group, k, upward, total):
-        snd, rcv, s_sem, r_sem, to, _ = ring_refs(upward)
-        far = int(k > REACH)
-        snd[group, k - 1] = total.astype(BF16)
+        snd, rcv, s_sem, r_sem, to, reach = ring_refs(upward)
+        slot = k - 1 if reach < 4 else ring_slot(k)
+        kind, step = (2, 1) if relayed(k) else (1, k - REACH) if k > REACH else (0, k)
+        snd[group, slot] = total.astype(BF16)
         remote(
-            snd.at[group, k - 1], rcv.at[group, k - 1], s_sem, r_sem.at[group, far],
-            to[(k - REACH if far else k) - 1],
+            snd.at[group, slot], rcv.at[group, slot], s_sem, r_sem.at[group, kind], to[step - 1]
         ).start()
 
-    def ring_wait(group, upward, first, count, far):
+    def ring_wait(group, upward, first, count, kind):
         _, rcv, s_sem, r_sem, to, _ = ring_refs(upward)
         some = rcv.at[group, pl.ds(first, count)]
-        remote(some, some, s_sem, r_sem.at[group, far], to[0]).wait_recv()
+        remote(some, some, s_sem, r_sem.at[group, kind], to[0]).wait_recv()
         return [rcv[group, first + k].astype(F32) for k in range(count)]
 
     def ring_start(group):
@@ -370,10 +378,27 @@
         )
         terms = dot(held, dkv_sh[:, group].reshape(LANES * rows, 2 * HEAD_DIM))
         prod[group] = terms.reshape(zs, feats, 2 * HEAD_DIM)
-        for k in range(hp, 0, -1):
-            for upward, reach in ((True, hp), (False, hm)):
-                if k <= reach and (k != REACH or reach <= REACH):
-                    ring_send(group, k, upward, prod[group, at_z(k if upward else -k)])
+        for k in range(hp, REACH, -1):
+            ring_both(group, k)
+
+    def ring_both(group, k):
+        for upward, reach in ((True, hp), (False, hm)):
+            if k <= reach and (k != REACH or reach <= REACH):
+                ring_send(group, k, upward, prod[group, at_z(k if upward else -k)])
+
+    def ring_near(group):
+        for k in range(min(REACH, hp), 0, -1):
+            if k != 2:
+                ring_both(group, k)
+
+    def ring_next(group):
+        for upward, reach in ((True, hp), (False, hm)):
+            if reach >= 2 and REACH >= 2:
+                total = prod[group, at_z(2 if upward else -2)]
+                if reach >= 3 and REACH > 3:
+                    (term,) = ring_wait(group, upward, 2 if reach < 4 else 3, 1, 2)
+                    total = total + term
+                ring_send(group, 2, upward, total)
 
     def ring_middle(group):
         for upward, reach in ((True, hp), (False, hm)):
@@ -387,7 +412,8 @@
         total = prod[group, z]
         for upward, reach in ((True, hp), (False, hm)):
             if reach > 0:
-                for term in ring_wait(group, upward, 0, min(REACH, reach), 0):
+                near = min(REACH, reach)
+                for term in ring_wait(group, upward, 0, near - int(near >= 3 and REACH > 3), 0):
                     total = total + term
         total = total * (1.0 / math.sqrt(rows * n_ctx))
         at_k, at_v = group * HEAD_DIM, (KV_HEADS + group) * HEAD_DIM
@@ -409,10 +435,10 @@
     with jax.named_scope("nt"):
         three = nt_sh.at[pl.ds(0, LANES - 1)]
         remote(three, three, nt_snd, nt_rcv, me_c).wait_recv()
+    with jax.named_scope("share1"):
+        share_start(1)
     with jax.named_scope("pass0"):
         share_pass(0)
-    with jax.named_scope("share1"):
-        share_start(1)
     shift_start(1, 0)
     shift_start(0, 1)
     with jax.named_scope("ring0"):
@@ -467,10 +493,12 @@
     stage("fill1", lambda: fill(1))
     stage("ring1", lambda: ring_start(1))
     stage("fill1", lambda: fill(2))
+    stage("near", lambda: (ring_near(0), ring_near(1)))
     stage("mid0", lambda: ring_middle(0))
     stage("fwd", lambda: shift_start(1, 1))
     stage("fill2", lambda: fill(2))
     stage("mid1", lambda: ring_middle(1))
+    stage("next", lambda: (ring_next(0), ring_next(1)))
     stage("end0", lambda: ring_end(0))
     stage("last", lambda: fill(len(todo)))
     stage("end1", lambda: ring_end(1))
@@ -527,7 +555,7 @@
         dma, dma, dma, dma, dma, dma((2,)),
         dma, dma((KV_HEADS,)), dma, dma((KV_HEADS,)),
         dma, dma((KV_HEADS, 2)),
-        dma, dma((KV_HEADS, 2)), dma, dma((KV_HEADS, 2)),
+        dma, dma((KV_HEADS, 3)), dma, dma((KV_HEADS, 3)),
     ]
     hbm = pl.BlockSpec(memory_space=pltpu.HBM)
     vmem = pl.BlockSpec(memory_space=pltpu.VMEM)

time: 70.6 us -> 68.8 us (0.975)
  Pallas kernels: 69.3 us -> 68.1 us
    pallas_call x1, Pallas kernels: 68.3 us -> 67.1 us  [per_device(): pl.pallas_call(functools.partial(kernel, n_pipe, n_ctx), out_shape=shapes...]
where the time goes in v4:
time: 68.8 us; the launch traced here: 68.7 us
  Pallas kernels  68.1 us (99%)
    pallas_call x1, Pallas kernels, per_device(): pl.pallas_call(functools.partial(kernel, n_pipe, n_ctx), out_shape=shapes...  67.1 us

profile of v4, /device:TPU:1, one launch (start us, length us, event | category | flops | bytes accessed | tf_op | source)
XLA Modules:
  0.0 68.7 jit_solution(1150721650696563283)
XLA Ops:
  0.6 67.1 %step.1 = (bf16[128,2048]{1,0:T(8,128)(2,1)S(1)}, bf16[128,2048]{1,0:T(8,128)(2,1)S(1)}, f32[32,512]{1,0:T(8,128)S(1)}) custom-call(bf16[128,2048]{1,0:T(8,128)(2,1)} %bitcast.8, bf16[128,2048]{1,0:T(8,128)(2,1)} %bitcast.9, bf16[128,2048]{1,0:T(8,128)(2,1)} %bitcast.10, bf16[128,2048]{1,0:T(8,128)(2,1)} %bitcast.11, bf16[32,512]{1,0:T(8,128)(2,1)} %bitcast.12), custom_call_target="tpu_custom_call" | custom-call | tf_op jit(solution)/shard_map/step/pallas_call | solution.py:567
  67.7 1.0 %store.1 = (bf16[128,2048]{1,0:T(8,128)(2,1)}, bf16[128,2048]{1,0:T(8,128)(2,1)}, f32[32,512]{1,0:T(8,128)}) custom-call(bf16[128,2048]{1,0:T(8,128)(2,1)S(1)} %get-tuple-element.9.go_v, bf16[128,2048]{1,0:T(8,128)(2,1)S(1)} %get-tuple-element.10.dq_v, f32[32,512]{1,0:T(8,128)S(1)} %get-tuple-element.11.wg_v), custom_call_target="tpu_custom_call" | custom-call | tf_op jit(solution)/shard_map/store/pallas_call | solution.py:581

commit v5 on v4

--- a/solution.py
+++ b/solution.py
@@ -488,9 +488,8 @@
         with jax.named_scope(name):
             act()
 
+    stage("pass1", lambda: share_pass(1))
     stage("fill0", lambda: fill(3))
-    stage("pass1", lambda: share_pass(1))
-    stage("fill1", lambda: fill(1))
     stage("ring1", lambda: ring_start(1))
     stage("fill1", lambda: fill(2))
     stage("near", lambda: (ring_near(0), ring_near(1)))

time: 68.8 us -> 68.9 us (level)
  no operation moved by 1% of the time
where the time goes in v5:
time: 68.9 us; the launch traced here: 68.7 us
  Pallas kernels  68.1 us (99%)
    pallas_call x1, Pallas kernels, per_device(): pl.pallas_call(functools.partial(kernel, n_pipe, n_ctx), out_shape=shapes...  67.1 us

profile of v5, /device:TPU:1, one launch (start us, length us, event | category | flops | bytes accessed | tf_op | source)
XLA Modules:
  0.0 68.7 jit_solution(4451853435816397673)
XLA Ops:
  0.6 67.1 %step.1 = (bf16[128,2048]{1,0:T(8,128)(2,1)S(1)}, bf16[128,2048]{1,0:T(8,128)(2,1)S(1)}, f32[32,512]{1,0:T(8,128)S(1)}) custom-call(bf16[128,2048]{1,0:T(8,128)(2,1)} %bitcast.8, bf16[128,2048]{1,0:T(8,128)(2,1)} %bitcast.9, bf16[128,2048]{1,0:T(8,128)(2,1)} %bitcast.10, bf16[128,2048]{1,0:T(8,128)(2,1)} %bitcast.11, bf16[32,512]{1,0:T(8,128)(2,1)} %bitcast.12), custom_call_target="tpu_custom_call" | custom-call | tf_op jit(solution)/shard_map/step/pallas_call | solution.py:566
  67.7 1.0 %store.1 = (bf16[128,2048]{1,0:T(8,128)(2,1)}, bf16[128,2048]{1,0:T(8,128)(2,1)}, f32[32,512]{1,0:T(8,128)}) custom-call(bf16[128,2048]{1,0:T(8,128)(2,1)S(1)} %get-tuple-element.9.go_v, bf16[128,2048]{1,0:T(8,128)(2,1)S(1)} %get-tuple-element.10.dq_v, f32[32,512]{1,0:T(8,128)S(1)} %get-tuple-element.11.wg_v), custom_call_target="tpu_custom_call" | custom-call | tf_op jit(solution)/shard_map/store/pallas_call | solution.py:580
